TPU v7x, 512 devices: a whole 4x4x16 slice. The times are simulated.
512 devices in a mesh: quad: 16 (over z_lo, core), gy: 8 (over y, z_hi), gx: 4 (over x).
Axes of the slice: x: 4, y: 4, z: 16 (z_hi: 2, z_lo: 8; z = z_hi * 8 + z_lo), core: 2. Of those that a mesh axis runs over, the one named last changes fastest.
Arguments:
- modes_now: bfloat16 [1024, 64, 512], P('quad', 'gy', 'gx'), may hold values from -4 to 4
- basis_rows: bfloat16 [4096, 1024], P('quad'), may hold values from -0.25 to 0.25
- quad_weights: float32 [4096], P('quad'), may hold values from 0.2 to 2
- germ_nodes: float32 [4096, 8], P('quad'), may hold values from -1.5 to 1.5
- log_fields: float32 [8, 64, 512], P(None, 'gy', 'gx'), may hold values from -1 to 1
- reaction_rates: float32 [4096], P('quad'), may hold values from 0.08 to 0.32
Outputs:
- modes_next: float32 [1024, 64, 512], P('quad', 'gy', 'gx')
All inputs are finite; a program needn't handle non-finite values.
Results may differ from a plain program's by a relative error of at most 0.02.
Values may be sent and summed in bfloat16 or wider, within the bound.
No kernel may reach another device: no remote copies, remote signals or barrier semaphores. Data moves between devices by JAX's collectives and lax.ppermute only.
A program may use at most 64 MiB of HBM per device.

v0:
```python
import itertools

import jax
import jax.numpy as jnp
from jax import lax
from jax.experimental import pallas as pl
from jax.experimental.pallas import tpu as pltpu
from jax.sharding import Mesh
from jax.sharding import PartitionSpec as P


STEP = 0.04
BF = jnp.bfloat16
F32 = jnp.float32
VM = pltpu.VMEM
OFFS = (0, -1, 1, 2)
ARRIVAL = tuple((o, i) for o, half in ((0, 0), (0, 2), (1, 0), (2, 0), (1, 2), (2, 2), (3, 0), (3, 2)) for i in (half, half + 1))
ALL = ("zl", "core", "y", "zh", "x")
SPLIT = (8, 2, 4, 2, 4)


def shift(moves):
    every = list(itertools.product(*map(range, SPLIT)))
    number = {at: i for i, at in enumerate(every)}
    pairs = ((number[at], number.get(moves(*at))) for at in every)
    return [(i, j) for i, j in pairs if j is not None]


def plane_shift(phase, step):
    def moves(zl, core, y, zh, x):
        if (core + phase) % 2 == 0:
            return zl, core, y, zh, (x + step) % 4
        return zl, core, (y + step) % 4, zh, x

    return shift(moves)


def shape(dims, kind):
    return jax.ShapeDtypeStruct(dims, kind)


def halves(low, high):
    lane = lax.broadcasted_iota(jnp.int32, low.shape, 1)
    return jnp.where(lane < 64, low, high)


def swapped(x):
    return pltpu.roll(x, 64, 1)


def rows_kernel(modes_ref, logs_ref, out_ref, scr_ref, log_ref):
    scr_ref[...] = modes_ref[...].astype(F32)
    log_ref[...] = logs_ref[...]
    upper = jnp.zeros((1, 128), jnp.int32) + lax.axis_index("zh") == 0
    for k in range(2):
        logs = jnp.where(upper, log_ref[pl.ds(k, 8, stride=8), :], log_ref[pl.ds(6 + k, 8, stride=8), :])
        high = logs.astype(BF).astype(F32)
        block = jnp.where(upper, scr_ref[pl.ds(k, 64, stride=8), :], scr_ref[pl.ds(6 + k, 64, stride=8), :])
        out_ref[k * 80 : k * 80 + 80, :] = jnp.concatenate([block, high, logs - high], axis=0).astype(BF)


def channels_kernel(modes_ref, logs_ref, chan_ref, scr_ref, log_ref):
    scr_ref[...] = modes_ref[...].astype(F32)
    log_ref[...] = logs_ref[...]
    zeros = jnp.zeros((48, 128), F32)
    for y in range(8):
        block = scr_ref[pl.ds(y, 64, stride=8), :]
        logs = log_ref[pl.ds(y, 8, stride=8), :]
        high = logs.astype(BF).astype(F32)
        chan_ref[y] = jnp.concatenate([block, high, logs - high, zeros], axis=0).T


def edges_kernel(chan_ref, got_ref, full_ref, last_ref, lead_ref):
    lower = lax.axis_index("zh")
    zeros = jnp.zeros((48, 128), F32)
    got = got_ref[...].astype(F32)
    for k in range(2):
        full_ref[8 - 8 * lower + k, 8:136, :] = jnp.concatenate([got[k * 80 : k * 80 + 80], zeros], axis=0).T
    for r in range(8):
        full_ref[2 * lower + r, 8:136, :] = chan_ref[r]
    for r in range(10):
        last_ref[r * 8 : r * 8 + 8] = full_ref[r, 128:136, :].astype(BF)
        lead_ref[r * 8 : r * 8 + 8] = full_ref[r, 8:16, :].astype(BF)


def log_rows(cell_ref, rows):
    lane = lax.broadcasted_iota(jnp.int32, (rows, 128), 1)
    logs = jnp.zeros((rows, 128), F32)
    for g in range(8):
        piece = pltpu.roll(cell_ref[g * rows : (g + 1) * rows, :], (g * 16 - 64) % 128, 1)
        logs = jnp.where((lane >= g * 16) & (lane < g * 16 + 16), piece, logs)
    return logs


def patches_kernel(full_ref, left_ref, right_ref, pars_ref, send_ref, wide_ref, cell_ref, scr_ref):
    left, right = left_ref[...].astype(F32), right_ref[...].astype(F32)
    for r in range(10):
        wide_ref[r, 0:8, :] = left[r * 8 : r * 8 + 8]
        wide_ref[r, 8:136, :] = full_ref[r, 8:136, :]
        wide_ref[r, 136:144, :] = right[r * 8 : r * 8 + 8]
    zh = lax.axis_index("zh")
    scr_ref[...] = jnp.zeros_like(scr_ref)
    for d in range(8):
        for r in range(8):
            cell_ref[r * 20 : r * 20 + 20, :] = wide_ref[2 * zh + r, 16 * d + 6 : 16 * d + 26, :]
        scr_ref[0:80, :] = halves(cell_ref[0:80, :], swapped(cell_ref[80:160, :]))
        scr_ref[80:100, :] = log_rows(cell_ref, 20)
        send_ref[zh * 8 + d] = scr_ref[...].astype(BF)
    pars = pars_ref[...]
    high = pars.astype(BF).astype(F32)
    scr_ref[56:76, :] = high
    scr_ref[76:96, :] = pars - high
    for d in range(8):
        for r in range(4):
            cell_ref[r * 20 : r * 20 + 20, :] = wide_ref[6 - 6 * zh + r, 16 * d + 6 : 16 * d + 26, :]
        scr_ref[0:40, :] = halves(cell_ref[0:40, :], swapped(cell_ref[40:80, :]))
        scr_ref[40:50, :] = log_rows(cell_ref, 10)
        send_ref[8 - 8 * zh + d] = scr_ref[...].astype(BF)


def coef_kernel(mine_ref, coef_ref, wr_ref, scr_ref, par_ref, log_ref):
    core, y, zh, x = (lax.axis_index(axis) for axis in ("core", "y", "zh", "x"))
    for z in range(8):
        scr_ref[z * 40 : (z + 1) * 40, :] = mine_ref[8 - 8 * zh + z].astype(F32)[56:96]
    sub = lax.broadcasted_iota(jnp.int32, (8, 128), 0)
    grp = lax.broadcasted_iota(jnp.int32, (8, 128), 1) // 16
    for v in range(10):
        for h in range(2):
            at = v * 2 + h
            got = scr_ref[pl.ds(at, 8, stride=40), :] + scr_ref[pl.ds(at + 20, 8, stride=40), :]
            for s in (1, 2, 4):
                up = pltpu.roll(pltpu.roll(got, 8 - s, 0), 16 * s, 1)
                down = pltpu.roll(pltpu.roll(got, s, 0), 128 - 16 * s, 1)
                mine, bit = (sub & s) > 0, (grp & s) > 0
                got = jnp.where(mine == bit, got, jnp.where(mine, down, up))
            par_ref[v, h * 8 : h * 8 + 8, :] = got
    same = mine_ref[zh * 8].astype(F32)
    same = same + pltpu.roll(same, 120, 1)
    other = mine_ref[8 - 8 * zh].astype(F32)
    other = other + pltpu.roll(other, 120, 1)
    for g in range(8):
        log_ref[40 + g * 20 : 60 + g * 20, :] = pltpu.roll(same, (128 - g * 16) % 128, 1)[80:100]
        at = g * 10 if g < 4 else 160 + g * 10
        log_ref[at : at + 10, :] = pltpu.roll(other, (128 - g * 16) % 128, 1)[40:50]
    cols = [log_ref[:, j : j + 1] for j in range(8)]
    for n, (o, i) in enumerate(ARRIVAL):
        dy, dx = jnp.where(core == 0, OFFS[o], OFFS[i]), jnp.where(core == 0, OFFS[i], OFFS[o])
        p = ((y + dy) & 3) * 4 + ((x + dx) & 3)
        for v in range(2):
            wr_ref[v, n : n + 1, :] = par_ref[v, pl.ds(p, 1), :]
        acc = cols[0] * par_ref[2, pl.ds(p, 1), :]
        for j in range(1, 8):
            acc = acc + cols[j] * par_ref[2 + j, pl.ds(p, 1), :]
        coef_ref[n] = jnp.exp(acc)


def state_kernel(mine_ref, theirs_ref, state_ref, scr_ref):
    first = jnp.zeros((1, 128), jnp.int32) + lax.axis_index("core") == 0
    zh = lax.axis_index("zh")
    for z in range(8):
        for at, rows, lo, hi in ((zh * 8 + z, 80, 40, 120), (8 - 8 * zh + z, 40, 0, 200)):
            mine, theirs = mine_ref[at].astype(F32)[0:rows], theirs_ref[at].astype(F32)[0:rows]
            zero, one = jnp.where(first, mine, theirs), jnp.where(first, theirs, mine)
            scr_ref[lo : lo + rows, :] = halves(zero, swapped(one))
            scr_ref[hi : hi + rows, :] = halves(swapped(zero), one)
        state_ref[:, z * 128 : (z + 1) * 128] = scr_ref[...].astype(BF)


def drive(f_ref, h, coef_ref, c, rows, skip, rate, weight):
    def f(d):
        return f_ref[h, 20 + d : 20 + d + rows, :]

    def k(d):
        return coef_ref[c, skip + 20 + d : skip + 20 + d + rows, :]

    mid, kmid = f(0), k(0)
    total = (kmid + k(-20)) * (f(-20) - mid)
    for d in (20, -1, 1):
        total = total + (kmid + k(d)) * (f(d) - mid)
    total = total + rate * (mid - mid * mid * mid)
    return (weight * total).astype(BF)


def sweep(state, basis_refs, coef_ref, wr_ref, f_ref, acc_ref, rows, skip, c=0):
    for ref in basis_refs:
        block = ref[...]
        field = lax.dot_general(state, block, (((1,), (1,)), ((), ())), preferred_element_type=F32)
        parts = []
        for h in range(2):
            f_ref[h, : field.shape[0], :] = field[:, h * 128 : (h + 1) * 128]
            weight, rate = wr_ref[0, c : c + 1, :], wr_ref[1, c : c + 1, :]
            parts.append(drive(f_ref, h, coef_ref, c, rows, skip, rate, weight))
            c += 1
        acc_ref[...] += jnp.dot(jnp.concatenate(parts, axis=1), block, preferred_element_type=F32)


def first_kernel(*refs):
    blocks, (state_ref, coef_ref, wr_ref, out_ref, f_ref, acc_ref) = refs[:8], refs[8:]
    acc_ref[...] = jnp.zeros_like(acc_ref)
    sweep(state_ref[...], blocks, coef_ref, wr_ref, f_ref, acc_ref, 200, 0)
    out_ref[...] = acc_ref[...].astype(BF)


def second_kernel(*refs):
    blocks, (state_ref, coef_ref, wr_ref, own_ref, other_ref, out_ref, f_ref, acc_ref) = refs[:8], refs[8:]
    total = own_ref[...].astype(F32) + other_ref[...].astype(F32)
    now = state_ref[...].astype(F32)[20:220]
    cell = lax.broadcasted_iota(jnp.int32, (200, 128), 0).astype(F32)
    row = jnp.floor((cell + 0.5) * 0.05)
    col = cell - 20.0 * row
    zl, _, y, zh, x = (lax.axis_index(axis) for axis in ALL)
    low = jnp.where((y == 0) & (zh == 0), 1.0, 0.0)
    high = jnp.where((y == 3) & (zh == 1), 8.0, 9.0)
    left = jnp.where((x == 0) & (zl == 0), 2.0, 0.0)
    right = jnp.where((x == 3) & (zl == 7), 17.0, 19.0)
    inside = (row >= low) & (row <= high) & (col >= left) & (col <= right)
    keep = jnp.where(inside, 1.0, 0.0)[:, 0:1]
    state = ((now + STEP * total) * keep).astype(BF)
    acc_ref[...] = jnp.zeros_like(acc_ref)
    sweep(state, blocks, coef_ref, wr_ref, f_ref, acc_ref, 160, 20)
    for z in range(8):
        for y in range(4):
            low = acc_ref[y * 20 + 2 : y * 20 + 18, z * 128 : (z + 1) * 128]
            high = acc_ref[y * 20 + 82 : y * 20 + 98, z * 128 : (z + 1) * 128]
            out_ref[2 * z, y * 16 : y * 16 + 16, :] = halves(low, swapped(high)).astype(BF)
            out_ref[2 * z + 1, y * 16 : y * 16 + 16, :] = halves(swapped(low), high).astype(BF)


def finish_kernel(back_ref, modes_ref, out_ref, scr_ref):
    for y in range(4):
        parts = [
            back_ref[2 * z, y * 16 : y * 16 + 16, :].astype(F32) + back_ref[2 * z + 1, y * 16 : y * 16 + 16, :].astype(F32)
            for z in range(8)
        ]
        turned = jnp.concatenate(parts, axis=0).T
        scr_ref[pl.ds(y, 64, stride=8), :] = turned[0:64]
        scr_ref[pl.ds(y + 4, 64, stride=8), :] = turned[64:128]
    out_ref[...] = modes_ref[...].astype(F32) + STEP * scr_ref[...]


SMEM = pl.BlockSpec(memory_space=pltpu.SMEM)
WHOLE = pl.BlockSpec(memory_space=pltpu.VMEM)


def call(kernel, outs, scratch, scalars, *args):
    specs = [SMEM] * scalars + [WHOLE] * (len(args) - scalars)
    if kernel in (first_kernel, second_kernel):
        args = [pltpu.with_memory_space_constraint(a, pltpu.VMEM) if a.size >= 1 << 17 else a for a in args]
    single = not isinstance(outs, (list, tuple))
    return pl.pallas_call(
        kernel,
        out_shape=outs,
        in_specs=specs,
        out_specs=WHOLE if single else [WHOLE] * len(outs),
        scratch_shapes=scratch,
        compiler_params=pltpu.CompilerParams(vmem_limit_bytes=20 << 20),
    )(*args)


def update(modes_now, basis_rows, quad_weights, germ_nodes, log_fields, reaction_rates):
    y, x = lax.axis_index("y"), lax.axis_index("x")

    part = lax.dynamic_slice_in_dim(basis_rows, (y * 4 + x) * 16, 16, axis=0)
    send = jnp.broadcast_to(part[None], (8, 16, 1024))
    shard = lax.all_to_all(send, "zl", 0, 0, tiled=True).reshape(128, 1024)

    modes, logs = modes_now.reshape(512, 128), log_fields.reshape(64, 128)
    scratch = [VM((512, 128), F32), VM((64, 128), F32)]
    rows = call(rows_kernel, shape((160, 128), BF), scratch, 0, modes, logs)

    def toward(zl, core, y, zh, x):
        return zl, core, y + 2 * zh - 1, zh, x

    got = lax.ppermute(rows, ALL, shift(toward))
    chan = call(channels_kernel, shape((8, 128, 128), F32), scratch, 0, modes, logs)
    full, last, lead = call(
        edges_kernel,
        [shape((10, 144, 128), F32), shape((80, 128), BF), shape((80, 128), BF)],
        [],
        0,
        chan,
        got,
    )
    right = [(i, i + 1) for i in range(3)]
    from_left = lax.ppermute(last, "x", right)
    from_right = lax.ppermute(lead, "x", [(j, i) for i, j in right])
    pars = jnp.concatenate([quad_weights[None], reaction_rates[None], germ_nodes.T], axis=0).reshape(20, 128)
    patch = call(
        patches_kernel,
        shape((16, 104, 128), BF),
        [VM((10, 144, 128), F32), VM((160, 128), F32), VM((104, 128), F32)],
        0,
        full,
        from_left,
        from_right,
        pars,
    )
    mine = lax.all_to_all(patch, ("zh", "zl"), 0, 0, tiled=True)
    theirs = lax.ppermute(mine, "core", [(0, 1), (1, 0)])

    fwd, bwd = plane_shift(0, 1), plane_shift(0, -1)
    less = lax.ppermute(shard, ALL, fwd)
    more = lax.ppermute(shard, ALL, bwd)
    near = jnp.concatenate([shard, less], axis=0)
    far = lax.ppermute(less, ALL, fwd)
    fwd, bwd = plane_shift(1, 1), plane_shift(1, -1)
    near_less = lax.ppermute(near, ALL, fwd)
    near_more = lax.ppermute(near, ALL, bwd)
    away = jnp.concatenate([more, far], axis=0)
    away_more = lax.ppermute(away, ALL, bwd)
    away_less = lax.ppermute(away, ALL, fwd)
    near_far = lax.ppermute(near_less, ALL, fwd)
    away_far = lax.ppermute(away_more, ALL, bwd)
    blocks = (near, away, near_less, near_more, away_less, away_more, near_far, away_far)

    coef, wr = call(
        coef_kernel,
        [shape((16, 240, 128), F32), shape((2, 16, 128), F32)],
        [VM((320, 128), F32), VM((10, 16, 128), F32), VM((240, 128), F32)],
        0,
        mine,
    )
    state = call(state_kernel, shape((240, 1024), BF), [VM((240, 128), F32)], 0, mine, theirs)
    scratch = [VM((2, 240, 128), F32), VM((200, 1024), F32)]
    own = call(first_kernel, shape((200, 1024), BF), scratch, 0, *blocks, state, coef, wr)
    other = lax.ppermute(own, "core", [(0, 1), (1, 0)])
    scratch = [VM((2, 200, 128), F32), VM((160, 1024), F32)]
    out = call(second_kernel, shape((16, 64, 128), BF), scratch, 0, *blocks, state, coef, wr, own, other)
    back = lax.all_to_all(out, ("zl", "core"), 0, 0, tiled=True)
    result = call(finish_kernel, shape((512, 128), F32), [VM((512, 128), F32)], 0, back, modes)
    return result.reshape(64, 8, 128)


def solution(mesh):
    fine = Mesh(mesh.devices.reshape(SPLIT), ALL)
    quad = ("zl", "core")
    in_specs = (P(quad, ("y", "zh"), "x"), P(quad, None), P(quad), P(quad, None), P(None, ("y", "zh"), "x"), P(quad))
    out_specs = P(quad, ("y", "zh"), "x")
    return jax.shard_map(update, mesh=fine, in_specs=in_specs, out_specs=out_specs, check_vma=False)
```

profile of v0, /device:TPU:1, one launch (start us, length us, event | category | flops | bytes accessed | tf_op | source)
XLA Modules:
  0.0 130.4 jit_solution(4138695265201194643)
XLA Ops:
  0.0 1.0 copy-done
  1.0 0.7 broadcast_in_dim.12
  1.8 13.1 %all-to-all-start = ((bf16[8,16,1024]{2,1,0:T(8,128)(2,1)}), bf16[8,16,1024]{2,1,0:T(8,128)(2,1)S(1)}, u32[]{:S(2)}, u32[]{:S(2)}) async-start(bf16[8,16,1024]{2,1,0:T(8,128)(2,1)} %broadcast_in_dim.12), calls=%async_computation | async-start | bytes 524288 | tf_op jit(solution)/shard_map/all_to_all | solution.py:265
  14.8 0.9 copy-done.1
  15.7 0.8 copy-done.3
  16.6 1.3 collective-permute-start.9
  18.1 3.5 %collective-permute-done.9.got_ref = bf16[160,128]{1,0:T(8,128)(2,1)S(1)} collective-permute-done((bf16[160,128]{1,0:T(8,128)(2,1)S(1)}, bf16[160,128]{1,0:T(8,128)(2,1)S(1)}, u32[]{:S(2)}, u32[]{:S(2)}) %collective-permute-start.9) | collective-permute-done | bytes 40992 | tf_op jit(solution)/shard_map/ppermute | solution.py:274
  21.7 3.1 %collective-permute-start.10 = (bf16[80,128]{1,0:T(8,128)(2,1)S(1)}, bf16[80,128]{1,0:T(8,128)(2,1)S(1)}, u32[]{:S(2)}, u32[]{:S(2)}) collective-permute-start(bf16[80,128]{1,0:T(8,128)(2,1)S(1)} %get-tuple-element.11), channel_id=1, source_target_pairs={{0,1},{1,2},{2,3},{4,5},{5,6},{6,7},{8,9},{9,10},{10,11},{12,13},{... | collective-permute-start | bytes 61448 | tf_op jit(solution)/shard_map/ppermute | solution.py:285
  24.9 1.3 collective-permute-start.11
  26.2 3.5 %collective-permute-done.11.right_ref = bf16[80,128]{1,0:T(8,128)(2,1)S(1)} collective-permute-done((bf16[80,128]{1,0:T(8,128)(2,1)S(1)}, bf16[80,128]{1,0:T(8,128)(2,1)S(1)}, u32[]{:S(2)}, u32[]{:S(2)}) %collective-permute-start.11) | collective-permute-done | bytes 20512 | tf_op jit(solution)/shard_map/ppermute | solution.py:286
  29.7 1.4 %shard_map.67 = bf16[16,104,128]{2,1,0:T(8,128)(2,1)} custom-call(f32[10,144,128]{2,1,0:T(8,128)S(1)} %get-tuple-element.10.full_ref, bf16[80,128]{1,0:T(8,128)(2,1)S(1)} %collective-permute-done.10.left_ref, bf16[80,128]{1,0:T(8,128)(2,1)S(1)} %collective-permute-done.11.right_ref, f32[20,128]{1,0:T(8,128)S(1)} %reshape.19.pars_ref), custom_call_target="tpu_custom_call" | custom-call | tf_op jit(solution)/shard_map/pallas_call | solution.py:250
  31.1 9.2 %all-to-all-start.1 = ((bf16[16,104,128]{2,1,0:T(8,128)(2,1)}), bf16[16,104,128]{2,1,0:T(8,128)(2,1)S(1)}, u32[]{:S(2)}, u32[]{:S(2)}) async-start(bf16[16,104,128]{2,1,0:T(8,128)(2,1)} %shard_map.67), calls=%async_computation.1 | async-start | bytes 851968 | tf_op jit(solution)/shard_map/all_to_all | solution.py:298
  40.3 3.2 %collective-permute-start = (bf16[128,1024]{1,0:T(8,128)(2,1)S(1)}, bf16[128,1024]{1,0:T(8,128)(2,1)S(1)}, u32[]{:S(2)}, u32[]{:S(2)}) collective-permute-start(bf16[128,1024]{1,0:T(8,128)(2,1)S(1)} %bitcast.12), channel_id=1, source_target_pairs={{0,1},{1,2},{2,3},{3,0},{4,5},{5,6},{6,7},{7,4},{8,9},{9,10},{10,1... | collective-permute-start | bytes 786440 | tf_op jit(solution)/shard_map/ppermute | solution.py:302
  43.5 3.3 %collective-permute-start.1 = (bf16[128,1024]{1,0:T(8,128)(2,1)S(1)}, bf16[128,1024]{1,0:T(8,128)(2,1)S(1)}, u32[]{:S(2)}, u32[]{:S(2)}) collective-permute-start(bf16[128,1024]{1,0:T(8,128)(2,1)S(1)} %bitcast.13), channel_id=1, source_target_pairs={{0,3},{1,0},{2,1},{3,2},{4,7},{5,4},{6,5},{7,6},{8,11},{9,8},{10,9... | collective-permute-start | bytes 786440 | tf_op jit(solution)/shard_map/ppermute | solution.py:303
  46.8 1.8 %collective-permute-done = bf16[128,1024]{1,0:T(8,128)(2,1)S(1)} collective-permute-done((bf16[128,1024]{1,0:T(8,128)(2,1)S(1)}, bf16[128,1024]{1,0:T(8,128)(2,1)S(1)}, u32[]{:S(2)}, u32[]{:S(2)}) %collective-permute-start) | collective-permute-done | bytes 262176 | tf_op jit(solution)/shard_map/ppermute | solution.py:302
  48.6 2.0 %collective-permute-start.2 = (bf16[128,1024]{1,0:T(8,128)(2,1)S(1)}, bf16[128,1024]{1,0:T(8,128)(2,1)S(1)}, u32[]{:S(2)}, u32[]{:S(2)}) collective-permute-start(bf16[128,1024]{1,0:T(8,128)(2,1)S(1)} %collective-permute-done), channel_id=1, source_target_pairs={{0,1},{1,2},{2,3},{3,0},{4,5},{5,6},{6,7},{7,4},{8,9},{9,10},{10,1... | collective-permute-start | bytes 786440 | tf_op jit(solution)/shard_map/ppermute | solution.py:305
  50.6 3.1 %collective-permute-start.3 = (bf16[256,1024]{1,0:T(8,128)(2,1)S(1)}, bf16[256,1024]{1,0:T(8,128)(2,1)S(1)}, u32[]{:S(2)}, u32[]{:S(2)}) collective-permute-start(bf16[256,1024]{1,0:T(8,128)(2,1)S(1)} %pad_maximum_fusion.refs_0_), channel_id=1, source_target_pairs={{0,8},{1,9},{2,10},{3,11},{4,12},{5,13},{6,14},{7,15},{8,16},{9,17... | collective-permute-start | bytes 1572872 | tf_op jit(solution)/shard_map/ppermute | solution.py:307
  53.8 3.4 %collective-permute-done.2 = bf16[128,1024]{1,0:T(8,128)(2,1)S(1)} collective-permute-done((bf16[128,1024]{1,0:T(8,128)(2,1)S(1)}, bf16[128,1024]{1,0:T(8,128)(2,1)S(1)}, u32[]{:S(2)}, u32[]{:S(2)}) %collective-permute-start.2) | collective-permute-done | bytes 262176 | tf_op jit(solution)/shard_map/ppermute | solution.py:305
  57.2 2.9 %collective-permute-start.6 = (bf16[256,1024]{1,0:T(8,128)(2,1)S(1)}, bf16[256,1024]{1,0:T(8,128)(2,1)S(1)}, u32[]{:S(2)}, u32[]{:S(2)}) collective-permute-start(bf16[256,1024]{1,0:T(8,128)(2,1)S(1)} %constant_dynamic-update-slice_fusion.refs_1_), channel_id=1, source_target_pairs={{0,24},{1,25},{2,26},{3,27},{4,28},{5,29},{6,30},{7,31},{8,0},{9,1... | collective-permute-start | bytes 1572872 | tf_op jit(solution)/shard_map/ppermute | solution.py:310
  60.2 3.6 %collective-permute-start.4 = (bf16[256,1024]{1,0:T(8,128)(2,1)S(1)}, bf16[256,1024]{1,0:T(8,128)(2,1)}, u32[]{:S(2)}, u32[]{:S(2)}) collective-permute-start(bf16[256,1024]{1,0:T(8,128)(2,1)S(1)} %pad_maximum_fusion.refs_0_), channel_id=1, source_target_pairs={{0,24},{1,25},{2,26},{3,27},{4,28},{5,29},{6,30},{7,31},{8,0},{9,1... | collective-permute-start | bytes 1572872 | tf_op jit(solution)/shard_map/ppermute | solution.py:308
  63.8 1.9 %collective-permute-start.5 = (bf16[256,1024]{1,0:T(8,128)(2,1)S(1)}, bf16[256,1024]{1,0:T(8,128)(2,1)}, u32[]{:S(2)}, u32[]{:S(2)}) collective-permute-start(bf16[256,1024]{1,0:T(8,128)(2,1)S(1)} %constant_dynamic-update-slice_fusion.refs_1_), channel_id=1, source_target_pairs={{0,8},{1,9},{2,10},{3,11},{4,12},{5,13},{6,14},{7,15},{8,16},{9,17... | collective-permute-start | bytes 1572872 | tf_op jit(solution)/shard_map/ppermute | solution.py:311
  65.8 2.1 %collective-permute-start.7 = (bf16[256,1024]{1,0:T(8,128)(2,1)S(1)}, bf16[256,1024]{1,0:T(8,128)(2,1)}, u32[]{:S(2)}, u32[]{:S(2)}) collective-permute-start(bf16[256,1024]{1,0:T(8,128)(2,1)S(1)} %collective-permute-done.3.refs_2_), channel_id=1, source_target_pairs={{0,8},{1,9},{2,10},{3,11},{4,12},{5,13},{6,14},{7,15},{8,16},{9,17... | collective-permute-start | bytes 1572872 | tf_op jit(solution)/shard_map/ppermute | solution.py:312
  67.9 4.4 %collective-permute-start.8 = (bf16[256,1024]{1,0:T(8,128)(2,1)S(1)}, bf16[256,1024]{1,0:T(8,128)(2,1)}, u32[]{:S(2)}, u32[]{:S(2)}) collective-permute-start(bf16[256,1024]{1,0:T(8,128)(2,1)S(1)} %collective-permute-done.6.refs_5_), channel_id=1, source_target_pairs={{0,24},{1,25},{2,26},{3,27},{4,28},{5,29},{6,30},{7,31},{8,0},{9,1... | collective-permute-start | bytes 1572872 | tf_op jit(solution)/shard_map/ppermute | solution.py:313
  72.3 11.8 %collective-permute-start.12 = (bf16[16,104,128]{2,1,0:T(8,128)(2,1)S(1)}, bf16[16,104,128]{2,1,0:T(8,128)(2,1)S(1)}, u32[]{:S(2)}, u32[]{:S(2)}) collective-permute-start(bf16[16,104,128]{2,1,0:T(8,128)(2,1)S(1)} %all-to-all-done.1.mine_ref), channel_id=1, source_target_pairs={{0,32},{32,0},{1,33},{33,1},{2,34},{34,2},{3,35},{35,3},{4,36},{36... | collective-permute-start | bytes 1277960 | tf_op jit(solution)/shard_map/ppermute | solution.py:299
  84.1 1.8 %shard_map.69 = (f32[16,240,128]{2,1,0:T(8,128)S(1)}, f32[2,16,128]{2,1,0:T(8,128)S(1)}) custom-call(bf16[16,104,128]{2,1,0:T(8,128)(2,1)S(1)} %all-to-all-done.1.mine_ref), custom_call_target="tpu_custom_call" | custom-call | tf_op jit(solution)/shard_map/pallas_call | solution.py:250
  85.8 0.2 shard_map.68.refs_8_
  86.1 4.7 %shard_map.70.refs_11_ = bf16[200,1024]{1,0:T(8,128)(2,1)S(1)} custom-call(bf16[256,1024]{1,0:T(8,128)(2,1)S(1)} %pad_maximum_fusion.refs_0_, bf16[256,1024]{1,0:T(8,128)(2,1)S(1)} %constant_dynamic-update-slice_fusion.refs_1_, bf16[256,1024]{1,0:T(8,128)(2,1)S(1)} %collective-permute-done.3.refs_2_, bf16[256,1024]{1,0:T(8,128)(2,1)} %collective-permute-done.4.refs_3_, ...), custom_call_target="tpu_custom_call" | custom-call | tf_op jit(solution)/shard_map/pallas_call | solution.py:250
  90.9 5.5 %collective-permute-start.13 = (bf16[200,1024]{1,0:T(8,128)(2,1)S(1)}, bf16[200,1024]{1,0:T(8,128)(2,1)S(1)}, u32[]{:S(2)}, u32[]{:S(2)}) collective-permute-start(bf16[200,1024]{1,0:T(8,128)(2,1)S(1)} %shard_map.70.refs_11_), channel_id=1, source_target_pairs={{0,32},{32,0},{1,33},{33,1},{2,34},{34,2},{3,35},{35,3},{4,36},{36... | collective-permute-start | bytes 1228808 | tf_op jit(solution)/shard_map/ppermute | solution.py:326
  96.4 1.4 %collective-permute-done.13.refs_12_ = bf16[200,1024]{1,0:T(8,128)(2,1)S(1)} collective-permute-done((bf16[200,1024]{1,0:T(8,128)(2,1)S(1)}, bf16[200,1024]{1,0:T(8,128)(2,1)S(1)}, u32[]{:S(2)}, u32[]{:S(2)}) %collective-permute-start.13) | collective-permute-done | bytes 409632 | tf_op jit(solution)/shard_map/ppermute | solution.py:326
  97.7 4.8 %shard_map.71 = bf16[16,64,128]{2,1,0:T(8,128)(2,1)S(1)} custom-call(bf16[256,1024]{1,0:T(8,128)(2,1)S(1)} %pad_maximum_fusion.refs_0_, bf16[256,1024]{1,0:T(8,128)(2,1)S(1)} %constant_dynamic-update-slice_fusion.refs_1_, bf16[256,1024]{1,0:T(8,128)(2,1)S(1)} %collective-permute-done.3.refs_2_, bf16[256,1024]{1,0:T(8,128)(2,1)} %collective-permute-done.4.refs_3_, ...), custom_call_target="tpu_custom_call" | custom-call | tf_op jit(solution)/shard_map/pallas_call | solution.py:250
  102.5 27.0 %all_to_all.15.back_ref = bf16[16,64,128]{2,1,0:T(8,128)(2,1)S(1)} all-to-all(bf16[16,64,128]{2,1,0:T(8,128)(2,1)S(1)} %shard_map.71), channel_id=1, replica_groups=mesh['zl'=8,'core'=2,'y'=4,'zh'=2,'x'=4] {'zl','core'}, dimensions={0} | all-to-all | bytes 524288 | tf_op jit(solution)/shard_map/all_to_all | solution.py:329
  129.5 0.9 shard_map.72
  (31 shorter events, 0.5 us)
Async XLA Ops:
  0.0 1.0 copy-start
  0.0 26.2 %copy-start.5 = (f32[256]{0:T(256)S(1)}, f32[256]{0:T(256)}, u32[]{:S(2)}) copy-start(f32[256]{0:T(256)} %param.11) | copy-start | bytes 3076
  0.0 26.2 %copy-start.4 = (f32[256,8]{0,1:T(8,128)S(1)}, f32[256,8]{0,1:T(8,128)}, u32[]{:S(2)}) copy-start(f32[256,8]{0,1:T(8,128)} %param.9) | copy-start | bytes 24580
  0.0 26.2 %copy-start.6 = (f32[256]{0:T(256)S(1)}, f32[256]{0:T(256)}, u32[]{:S(2)}) copy-start(f32[256]{0:T(256)} %param.8) | copy-start | bytes 3076
  1.8 29.3 %all-to-all-start = ((bf16[8,16,1024]{2,1,0:T(8,128)(2,1)}), bf16[8,16,1024]{2,1,0:T(8,128)(2,1)S(1)}, u32[]{:S(2)}, u32[]{:S(2)}) async-start(bf16[8,16,1024]{2,1,0:T(8,128)(2,1)} %broadcast_in_dim.12), calls=%async_computation | async-start | bytes 524288 | tf_op jit(solution)/shard_map/all_to_all | solution.py:265
  14.8 0.9 copy-start.1
  15.7 0.8 copy-start.3
  16.6 5.0 %collective-permute-start.9 = (bf16[160,128]{1,0:T(8,128)(2,1)S(1)}, bf16[160,128]{1,0:T(8,128)(2,1)S(1)}, u32[]{:S(2)}, u32[]{:S(2)}) collective-permute-start(bf16[160,128]{1,0:T(8,128)(2,1)S(1)} %shard_map.65), channel_id=1, source_target_pairs={{4,12},{5,13},{6,14},{7,15},{8,0},{9,1},{10,2},{11,3},{12,20},{13,... | collective-permute-start | bytes 122888 | tf_op jit(solution)/shard_map/ppermute | solution.py:274
  21.7 4.5 %collective-permute-start.10 = (bf16[80,128]{1,0:T(8,128)(2,1)S(1)}, bf16[80,128]{1,0:T(8,128)(2,1)S(1)}, u32[]{:S(2)}, u32[]{:S(2)}) collective-permute-start(bf16[80,128]{1,0:T(8,128)(2,1)S(1)} %get-tuple-element.11), channel_id=1, source_target_pairs={{0,1},{1,2},{2,3},{4,5},{5,6},{6,7},{8,9},{9,10},{10,11},{12,13},{... | collective-permute-start | bytes 61448 | tf_op jit(solution)/shard_map/ppermute | solution.py:285
  24.9 4.8 %collective-permute-start.11 = (bf16[80,128]{1,0:T(8,128)(2,1)S(1)}, bf16[80,128]{1,0:T(8,128)(2,1)S(1)}, u32[]{:S(2)}, u32[]{:S(2)}) collective-permute-start(bf16[80,128]{1,0:T(8,128)(2,1)S(1)} %get-tuple-element.12), channel_id=1, source_target_pairs={{1,0},{2,1},{3,2},{5,4},{6,5},{7,6},{9,8},{10,9},{11,10},{13,12},{... | collective-permute-start | bytes 61448 | tf_op jit(solution)/shard_map/ppermute | solution.py:286
  31.1 41.2 %all-to-all-start.1 = ((bf16[16,104,128]{2,1,0:T(8,128)(2,1)}), bf16[16,104,128]{2,1,0:T(8,128)(2,1)S(1)}, u32[]{:S(2)}, u32[]{:S(2)}) async-start(bf16[16,104,128]{2,1,0:T(8,128)(2,1)} %shard_map.67), calls=%async_computation.1 | async-start | bytes 851968 | tf_op jit(solution)/shard_map/all_to_all | solution.py:298
  40.3 8.3 %collective-permute-start = (bf16[128,1024]{1,0:T(8,128)(2,1)S(1)}, bf16[128,1024]{1,0:T(8,128)(2,1)S(1)}, u32[]{:S(2)}, u32[]{:S(2)}) collective-permute-start(bf16[128,1024]{1,0:T(8,128)(2,1)S(1)} %bitcast.12), channel_id=1, source_target_pairs={{0,1},{1,2},{2,3},{3,0},{4,5},{5,6},{6,7},{7,4},{8,9},{9,10},{10,1... | collective-permute-start | bytes 786440 | tf_op jit(solution)/shard_map/ppermute | solution.py:302
  43.5 10.3 %collective-permute-start.1 = (bf16[128,1024]{1,0:T(8,128)(2,1)S(1)}, bf16[128,1024]{1,0:T(8,128)(2,1)S(1)}, u32[]{:S(2)}, u32[]{:S(2)}) collective-permute-start(bf16[128,1024]{1,0:T(8,128)(2,1)S(1)} %bitcast.13), channel_id=1, source_target_pairs={{0,3},{1,0},{2,1},{3,2},{4,7},{5,4},{6,5},{7,6},{8,11},{9,8},{10,9... | collective-permute-start | bytes 786440 | tf_op jit(solution)/shard_map/ppermute | solution.py:303
  48.6 8.6 %collective-permute-start.2 = (bf16[128,1024]{1,0:T(8,128)(2,1)S(1)}, bf16[128,1024]{1,0:T(8,128)(2,1)S(1)}, u32[]{:S(2)}, u32[]{:S(2)}) collective-permute-start(bf16[128,1024]{1,0:T(8,128)(2,1)S(1)} %collective-permute-done), channel_id=1, source_target_pairs={{0,1},{1,2},{2,3},{3,0},{4,5},{5,6},{6,7},{7,4},{8,9},{9,10},{10,1... | collective-permute-start | bytes 786440 | tf_op jit(solution)/shard_map/ppermute | solution.py:305
  50.6 15.1 %collective-permute-start.3 = (bf16[256,1024]{1,0:T(8,128)(2,1)S(1)}, bf16[256,1024]{1,0:T(8,128)(2,1)S(1)}, u32[]{:S(2)}, u32[]{:S(2)}) collective-permute-start(bf16[256,1024]{1,0:T(8,128)(2,1)S(1)} %pad_maximum_fusion.refs_0_), channel_id=1, source_target_pairs={{0,8},{1,9},{2,10},{3,11},{4,12},{5,13},{6,14},{7,15},{8,16},{9,17... | collective-permute-start | bytes 1572872 | tf_op jit(solution)/shard_map/ppermute | solution.py:307
  57.2 10.6 %collective-permute-start.6 = (bf16[256,1024]{1,0:T(8,128)(2,1)S(1)}, bf16[256,1024]{1,0:T(8,128)(2,1)S(1)}, u32[]{:S(2)}, u32[]{:S(2)}) collective-permute-start(bf16[256,1024]{1,0:T(8,128)(2,1)S(1)} %constant_dynamic-update-slice_fusion.refs_1_), channel_id=1, source_target_pairs={{0,24},{1,25},{2,26},{3,27},{4,28},{5,29},{6,30},{7,31},{8,0},{9,1... | collective-permute-start | bytes 1572872 | tf_op jit(solution)/shard_map/ppermute | solution.py:310
  60.2 25.9 %collective-permute-start.4 = (bf16[256,1024]{1,0:T(8,128)(2,1)S(1)}, bf16[256,1024]{1,0:T(8,128)(2,1)}, u32[]{:S(2)}, u32[]{:S(2)}) collective-permute-start(bf16[256,1024]{1,0:T(8,128)(2,1)S(1)} %pad_maximum_fusion.refs_0_), channel_id=1, source_target_pairs={{0,24},{1,25},{2,26},{3,27},{4,28},{5,29},{6,30},{7,31},{8,0},{9,1... | collective-permute-start | bytes 1572872 | tf_op jit(solution)/shard_map/ppermute | solution.py:308
  63.8 22.3 %collective-permute-start.5 = (bf16[256,1024]{1,0:T(8,128)(2,1)S(1)}, bf16[256,1024]{1,0:T(8,128)(2,1)}, u32[]{:S(2)}, u32[]{:S(2)}) collective-permute-start(bf16[256,1024]{1,0:T(8,128)(2,1)S(1)} %constant_dynamic-update-slice_fusion.refs_1_), channel_id=1, source_target_pairs={{0,8},{1,9},{2,10},{3,11},{4,12},{5,13},{6,14},{7,15},{8,16},{9,17... | collective-permute-start | bytes 1572872 | tf_op jit(solution)/shard_map/ppermute | solution.py:311
  65.8 20.4 %collective-permute-start.7 = (bf16[256,1024]{1,0:T(8,128)(2,1)S(1)}, bf16[256,1024]{1,0:T(8,128)(2,1)}, u32[]{:S(2)}, u32[]{:S(2)}) collective-permute-start(bf16[256,1024]{1,0:T(8,128)(2,1)S(1)} %collective-permute-done.3.refs_2_), channel_id=1, source_target_pairs={{0,8},{1,9},{2,10},{3,11},{4,12},{5,13},{6,14},{7,15},{8,16},{9,17... | collective-permute-start | bytes 1572872 | tf_op jit(solution)/shard_map/ppermute | solution.py:312
  67.9 18.3 %collective-permute-start.8 = (bf16[256,1024]{1,0:T(8,128)(2,1)S(1)}, bf16[256,1024]{1,0:T(8,128)(2,1)}, u32[]{:S(2)}, u32[]{:S(2)}) collective-permute-start(bf16[256,1024]{1,0:T(8,128)(2,1)S(1)} %collective-permute-done.6.refs_5_), channel_id=1, source_target_pairs={{0,24},{1,25},{2,26},{3,27},{4,28},{5,29},{6,30},{7,31},{8,0},{9,1... | collective-permute-start | bytes 1572872 | tf_op jit(solution)/shard_map/ppermute | solution.py:313
  72.3 13.5 %collective-permute-start.12 = (bf16[16,104,128]{2,1,0:T(8,128)(2,1)S(1)}, bf16[16,104,128]{2,1,0:T(8,128)(2,1)S(1)}, u32[]{:S(2)}, u32[]{:S(2)}) collective-permute-start(bf16[16,104,128]{2,1,0:T(8,128)(2,1)S(1)} %all-to-all-done.1.mine_ref), channel_id=1, source_target_pairs={{0,32},{32,0},{1,33},{33,1},{2,34},{34,2},{3,35},{35,3},{4,36},{36... | collective-permute-start | bytes 1277960 | tf_op jit(solution)/shard_map/ppermute | solution.py:299
  90.8 38.7 %copy-start.2 = (bf16[64,8,128]{2,1,0:T(8,128)(2,1)S(1)}, bf16[64,8,128]{2,1,0:T(8,128)(2,1)}, u32[]{:S(2)}) copy-start(bf16[64,8,128]{2,1,0:T(8,128)(2,1)} %param.6) | copy-start | bytes 393220
  90.9 6.9 %collective-permute-start.13 = (bf16[200,1024]{1,0:T(8,128)(2,1)S(1)}, bf16[200,1024]{1,0:T(8,128)(2,1)S(1)}, u32[]{:S(2)}, u32[]{:S(2)}) collective-permute-start(bf16[200,1024]{1,0:T(8,128)(2,1)S(1)} %shard_map.70.refs_11_), channel_id=1, source_target_pairs={{0,32},{32,0},{1,33},{33,1},{2,34},{34,2},{3,35},{35,3},{4,36},{36... | collective-permute-start | bytes 1228808 | tf_op jit(solution)/shard_map/ppermute | solution.py:326
where the time goes:
time: 131 us; the launch traced here: 130 us
  starting transfers between devices  71.8 us (55%)
  blocking collectives  27 us (21%)
  Pallas kernels  14.2 us (11%)
  waiting for transfers between devices  13.6 us (10%)
  local copies, waits for them, and re-layouts  3.47 us (3%)
    all_to_all x1, blocking collectives, update(): back = lax.all_to_all(out, ('zl', 'core'), 0, 0, tiled=True)  27 us
    pallas_call x9, Pallas kernels, call(): pl.pallas_call(kernel, out_shape=outs, in_specs=specs, out_specs=WHOLE if...  14.2 us
    all_to_all x1, starting transfers between devices, update(): shard = lax.all_to_all(send, 'zl', 0, 0, tiled=True).reshape(128, 1024)  13.1 us
    ppermute x1, starting transfers between devices, update(): theirs = lax.ppermute(mine, 'core', [(0, 1), (1, 0)])  11.8 us
    all_to_all x1, starting transfers between devices, update(): mine = lax.all_to_all(patch, ('zh', 'zl'), 0, 0, tiled=True)  9.16 us
    ppermute x1, starting transfers between devices, update(): other = lax.ppermute(own, 'core', [(0, 1), (1, 0)])  5.52 us
    ppermute x1, starting transfers between devices, update(): away_far = lax.ppermute(away_more, ALL, bwd)  4.41 us
    ppermute x1, starting transfers between devices, update(): near_more = lax.ppermute(near, ALL, bwd)  3.65 us
  transfers between devices with their start and end apart: 16, of which 5 were waited for; matrix products, arithmetic and copies ran while one was open for 0% of the time, Pallas kernels for 3%

commit v1 on v0

--- a/solution.py
+++ b/solution.py
@@ -202,7 +202,7 @@
 
 
 def second_kernel(*refs):
-    blocks, (state_ref, coef_ref, wr_ref, own_ref, other_ref, out_ref, f_ref, acc_ref) = refs[:8], refs[8:]
+    blocks, (state_ref, coef_ref, wr_ref, own_ref, other_ref, kept_ref, sent_ref, f_ref, acc_ref) = refs[:8], refs[8:]
     total = own_ref[...].astype(F32) + other_ref[...].astype(F32)
     now = state_ref[...].astype(F32)[20:220]
     cell = lax.broadcasted_iota(jnp.int32, (200, 128), 0).astype(F32)
@@ -218,19 +218,24 @@
     state = ((now + STEP * total) * keep).astype(BF)
     acc_ref[...] = jnp.zeros_like(acc_ref)
     sweep(state, blocks, coef_ref, wr_ref, f_ref, acc_ref, 160, 20)
+    first = jnp.zeros((1, 128), jnp.int32) + lax.axis_index("core") == 0
     for z in range(8):
         for y in range(4):
             low = acc_ref[y * 20 + 2 : y * 20 + 18, z * 128 : (z + 1) * 128]
             high = acc_ref[y * 20 + 82 : y * 20 + 98, z * 128 : (z + 1) * 128]
-            out_ref[2 * z, y * 16 : y * 16 + 16, :] = halves(low, swapped(high)).astype(BF)
-            out_ref[2 * z + 1, y * 16 : y * 16 + 16, :] = halves(swapped(low), high).astype(BF)
+            zero, one = halves(low, swapped(high)), halves(swapped(low), high)
+            kept_ref[z, y * 16 : y * 16 + 16, :] = jnp.where(first, zero, one)
+            sent_ref[z, y * 16 : y * 16 + 16, :] = jnp.where(first, one, zero).astype(BF)
+
+
+def add_kernel(kept_ref, got_ref, out_ref):
+    out_ref[...] = (kept_ref[...] + got_ref[...].astype(F32)).astype(BF)
 
 
 def finish_kernel(back_ref, modes_ref, out_ref, scr_ref):
     for y in range(4):
         parts = [
-            back_ref[2 * z, y * 16 : y * 16 + 16, :].astype(F32) + back_ref[2 * z + 1, y * 16 : y * 16 + 16, :].astype(F32)
-            for z in range(8)
+            back_ref[z, y * 16 : y * 16 + 16, :].astype(F32) for z in range(8)
         ]
         turned = jnp.concatenate(parts, axis=0).T
         scr_ref[pl.ds(y, 64, stride=8), :] = turned[0:64]
@@ -302,7 +307,7 @@
     less = lax.ppermute(shard, ALL, fwd)
     more = lax.ppermute(shard, ALL, bwd)
     near = jnp.concatenate([shard, less], axis=0)
-    far = lax.ppermute(less, ALL, fwd)
+    far = lax.ppermute(shard, ALL, plane_shift(0, 2))
     fwd, bwd = plane_shift(1, 1), plane_shift(1, -1)
     near_less = lax.ppermute(near, ALL, fwd)
     near_more = lax.ppermute(near, ALL, bwd)
@@ -325,8 +330,11 @@
     own = call(first_kernel, shape((200, 1024), BF), scratch, 0, *blocks, state, coef, wr)
     other = lax.ppermute(own, "core", [(0, 1), (1, 0)])
     scratch = [VM((2, 200, 128), F32), VM((160, 1024), F32)]
-    out = call(second_kernel, shape((16, 64, 128), BF), scratch, 0, *blocks, state, coef, wr, own, other)
-    back = lax.all_to_all(out, ("zl", "core"), 0, 0, tiled=True)
+    outs = [shape((8, 64, 128), F32), shape((8, 64, 128), BF)]
+    kept, sent = call(second_kernel, outs, scratch, 0, *blocks, state, coef, wr, own, other)
+    got = lax.ppermute(sent, "core", [(0, 1), (1, 0)])
+    out = call(add_kernel, shape((8, 64, 128), BF), [], 0, kept, got)
+    back = lax.all_to_all(out, "zl", 0, 0, tiled=True)
     result = call(finish_kernel, shape((512, 128), F32), [VM((512, 128), F32)], 0, back, modes)
     return result.reshape(64, 8, 128)
 

time: 131 us -> 127 us (0.969)
  blocking collectives: 27 us -> 19.4 us
  starting transfers between devices: 71.8 us -> 76.1 us
  waiting for transfers between devices: 13.6 us -> 11.9 us
    all_to_all x1, blocking collectives: 27 us -> 19.4 us  [update(): back = lax.all_to_all(out, 'zl', 0, 0, tiled=True)]
    ppermute x1 -> x2, starting transfers between devices: 1.98 us -> 5.89 us  [the longest x1 3.61 us: update(): far = lax.ppermute(shard, ALL, plane_shift(0, 2))]
    ppermute x1, waiting for transfers between devices: 1.82 us -> 0.01 us  [update(): less = lax.ppermute(shard, ALL, fwd)]
    ppermute x1, starting transfers between devices: 5.52 us -> 6.98 us  [update(): other = lax.ppermute(own, 'core', [(0, 1), (1, 0)])]
    ppermute x1 -> x2, waiting for transfers between devices: 3.41 us -> 3.04 us  [the longest x1 2.07 us: update(): far = lax.ppermute(shard, ALL, plane_shift(0, 2))]
    pallas_call x9 -> x10, Pallas kernels: 14.2 us -> 14.2 us  [call(): pl.pallas_call(kernel, out_shape=outs, in_specs=specs, out_specs=WHOLE if...]
  transfers between devices with their start and end apart: 16 -> 17, of which waited for: 5 -> 6; matrix products, arithmetic and copies ran while one was open for 0% -> 0% of each run, Pallas kernels for 3% -> 3%
where the time goes in v1:
time: 127 us; the launch traced here: 125 us
  starting transfers between devices  76.1 us (60%)
  blocking collectives  19.4 us (15%)
  Pallas kernels  14.2 us (11%)
  waiting for transfers between devices  11.9 us (9%)
  local copies, waits for them, and re-layouts  3.47 us (3%)
    all_to_all x1, blocking collectives, update(): back = lax.all_to_all(out, 'zl', 0, 0, tiled=True)  19.4 us
    pallas_call x10, Pallas kernels, call(): pl.pallas_call(kernel, out_shape=outs, in_specs=specs, out_specs=WHOLE if...  14.2 us
    all_to_all x1, starting transfers between devices, update(): shard = lax.all_to_all(send, 'zl', 0, 0, tiled=True).reshape(128, 1024)  13.1 us
    ppermute x1, starting transfers between devices, update(): theirs = lax.ppermute(mine, 'core', [(0, 1), (1, 0)])  10.7 us
    all_to_all x1, starting transfers between devices, update(): mine = lax.all_to_all(patch, ('zh', 'zl'), 0, 0, tiled=True)  9.16 us
    ppermute x1, starting transfers between devices, update(): other = lax.ppermute(own, 'core', [(0, 1), (1, 0)])  6.98 us
    ppermute x1, starting transfers between devices, update(): away_far = lax.ppermute(away_more, ALL, bwd)  4.57 us
    ppermute x1, starting transfers between devices, update(): near_more = lax.ppermute(near, ALL, bwd)  3.65 us
  transfers between devices with their start and end apart: 17, of which 6 were waited for; matrix products, arithmetic and copies ran while one was open for 0% of the time, Pallas kernels for 3%

profile of v1, /device:TPU:1, one launch (start us, length us, event | category | flops | bytes accessed | tf_op | source)
XLA Modules:
  0.0 125.4 jit_solution(11315051422020018131)
XLA Ops:
  0.0 1.0 copy-done
  1.0 0.7 broadcast_in_dim.12
  1.8 13.1 %all-to-all-start = ((bf16[8,16,1024]{2,1,0:T(8,128)(2,1)}), bf16[8,16,1024]{2,1,0:T(8,128)(2,1)S(1)}, u32[]{:S(2)}, u32[]{:S(2)}) async-start(bf16[8,16,1024]{2,1,0:T(8,128)(2,1)} %broadcast_in_dim.12), calls=%async_computation | async-start | bytes 524288 | tf_op jit(solution)/shard_map/all_to_all | solution.py:270
  14.8 0.9 copy-done.1
  15.7 0.8 copy-done.3
  16.6 1.3 %collective-permute-start.9 = (bf16[160,128]{1,0:T(8,128)(2,1)S(1)}, bf16[160,128]{1,0:T(8,128)(2,1)S(1)}, u32[]{:S(2)}, u32[]{:S(2)}) collective-permute-start(bf16[160,128]{1,0:T(8,128)(2,1)S(1)} %shard_map.65), channel_id=1, source_target_pairs={{4,12},{5,13},{6,14},{7,15},{8,0},{9,1},{10,2},{11,3},{12,20},{13,... | collective-permute-start | bytes 122888 | tf_op jit(solution)/shard_map/ppermute | solution.py:279
  18.1 3.5 %collective-permute-done.9.got_ref = bf16[160,128]{1,0:T(8,128)(2,1)S(1)} collective-permute-done((bf16[160,128]{1,0:T(8,128)(2,1)S(1)}, bf16[160,128]{1,0:T(8,128)(2,1)S(1)}, u32[]{:S(2)}, u32[]{:S(2)}) %collective-permute-start.9) | collective-permute-done | bytes 40992 | tf_op jit(solution)/shard_map/ppermute | solution.py:279
  21.7 3.1 %collective-permute-start.10 = (bf16[80,128]{1,0:T(8,128)(2,1)S(1)}, bf16[80,128]{1,0:T(8,128)(2,1)S(1)}, u32[]{:S(2)}, u32[]{:S(2)}) collective-permute-start(bf16[80,128]{1,0:T(8,128)(2,1)S(1)} %get-tuple-element.13), channel_id=1, source_target_pairs={{0,1},{1,2},{2,3},{4,5},{5,6},{6,7},{8,9},{9,10},{10,11},{12,13},{... | collective-permute-start | bytes 61448 | tf_op jit(solution)/shard_map/ppermute | solution.py:290
  24.9 1.3 %collective-permute-start.11 = (bf16[80,128]{1,0:T(8,128)(2,1)S(1)}, bf16[80,128]{1,0:T(8,128)(2,1)S(1)}, u32[]{:S(2)}, u32[]{:S(2)}) collective-permute-start(bf16[80,128]{1,0:T(8,128)(2,1)S(1)} %get-tuple-element.14), channel_id=1, source_target_pairs={{1,0},{2,1},{3,2},{5,4},{6,5},{7,6},{9,8},{10,9},{11,10},{13,12},{... | collective-permute-start | bytes 61448 | tf_op jit(solution)/shard_map/ppermute | solution.py:291
  26.2 3.5 %collective-permute-done.11.right_ref = bf16[80,128]{1,0:T(8,128)(2,1)S(1)} collective-permute-done((bf16[80,128]{1,0:T(8,128)(2,1)S(1)}, bf16[80,128]{1,0:T(8,128)(2,1)S(1)}, u32[]{:S(2)}, u32[]{:S(2)}) %collective-permute-start.11) | collective-permute-done | bytes 20512 | tf_op jit(solution)/shard_map/ppermute | solution.py:291
  29.7 1.4 %shard_map.67 = bf16[16,104,128]{2,1,0:T(8,128)(2,1)} custom-call(f32[10,144,128]{2,1,0:T(8,128)S(1)} %get-tuple-element.12.full_ref, bf16[80,128]{1,0:T(8,128)(2,1)S(1)} %collective-permute-done.10.left_ref, bf16[80,128]{1,0:T(8,128)(2,1)S(1)} %collective-permute-done.11.right_ref, f32[20,128]{1,0:T(8,128)S(1)} %reshape.19.pars_ref), custom_call_target="tpu_custom_call" | custom-call | tf_op jit(solution)/shard_map/pallas_call | solution.py:255
  31.1 9.2 %all-to-all-start.1 = ((bf16[16,104,128]{2,1,0:T(8,128)(2,1)}), bf16[16,104,128]{2,1,0:T(8,128)(2,1)S(1)}, u32[]{:S(2)}, u32[]{:S(2)}) async-start(bf16[16,104,128]{2,1,0:T(8,128)(2,1)} %shard_map.67), calls=%async_computation.1 | async-start | bytes 851968 | tf_op jit(solution)/shard_map/all_to_all | solution.py:303
  40.3 3.2 %collective-permute-start = (bf16[128,1024]{1,0:T(8,128)(2,1)S(1)}, bf16[128,1024]{1,0:T(8,128)(2,1)S(1)}, u32[]{:S(2)}, u32[]{:S(2)}) collective-permute-start(bf16[128,1024]{1,0:T(8,128)(2,1)S(1)} %bitcast.12), channel_id=1, source_target_pairs={{0,1},{1,2},{2,3},{3,0},{4,5},{5,6},{6,7},{7,4},{8,9},{9,10},{10,1... | collective-permute-start | bytes 786440 | tf_op jit(solution)/shard_map/ppermute | solution.py:307
  43.5 3.3 %collective-permute-start.1 = (bf16[128,1024]{1,0:T(8,128)(2,1)S(1)}, bf16[128,1024]{1,0:T(8,128)(2,1)S(1)}, u32[]{:S(2)}, u32[]{:S(2)}) collective-permute-start(bf16[128,1024]{1,0:T(8,128)(2,1)S(1)} %bitcast.13), channel_id=1, source_target_pairs={{0,3},{1,0},{2,1},{3,2},{4,7},{5,4},{6,5},{7,6},{8,11},{9,8},{10,9... | collective-permute-start | bytes 786440 | tf_op jit(solution)/shard_map/ppermute | solution.py:308
  46.8 3.6 %collective-permute-start.2 = (bf16[128,1024]{1,0:T(8,128)(2,1)S(1)}, bf16[128,1024]{1,0:T(8,128)(2,1)S(1)}, u32[]{:S(2)}, u32[]{:S(2)}) collective-permute-start(bf16[128,1024]{1,0:T(8,128)(2,1)S(1)} %bitcast.14), channel_id=1, source_target_pairs={{0,2},{1,3},{2,0},{3,1},{4,6},{5,7},{6,4},{7,5},{8,10},{9,11},{10,... | collective-permute-start | bytes 786440 | tf_op jit(solution)/shard_map/ppermute | solution.py:310
  50.5 3.1 %collective-permute-start.3 = (bf16[256,1024]{1,0:T(8,128)(2,1)S(1)}, bf16[256,1024]{1,0:T(8,128)(2,1)S(1)}, u32[]{:S(2)}, u32[]{:S(2)}) collective-permute-start(bf16[256,1024]{1,0:T(8,128)(2,1)S(1)} %pad_maximum_fusion.refs_0_), channel_id=1, source_target_pairs={{0,8},{1,9},{2,10},{3,11},{4,12},{5,13},{6,14},{7,15},{8,16},{9,17... | collective-permute-start | bytes 1572872 | tf_op jit(solution)/shard_map/ppermute | solution.py:312
  53.6 2.1 %collective-permute-done.2 = bf16[128,1024]{1,0:T(8,128)(2,1)S(1)} collective-permute-done((bf16[128,1024]{1,0:T(8,128)(2,1)S(1)}, bf16[128,1024]{1,0:T(8,128)(2,1)S(1)}, u32[]{:S(2)}, u32[]{:S(2)}) %collective-permute-start.2) | collective-permute-done | bytes 262176 | tf_op jit(solution)/shard_map/ppermute | solution.py:310
  55.7 2.9 %collective-permute-start.6 = (bf16[256,1024]{1,0:T(8,128)(2,1)S(1)}, bf16[256,1024]{1,0:T(8,128)(2,1)S(1)}, u32[]{:S(2)}, u32[]{:S(2)}) collective-permute-start(bf16[256,1024]{1,0:T(8,128)(2,1)S(1)} %constant_dynamic-update-slice_fusion.refs_1_), channel_id=1, source_target_pairs={{0,24},{1,25},{2,26},{3,27},{4,28},{5,29},{6,30},{7,31},{8,0},{9,1... | collective-permute-start | bytes 1572872 | tf_op jit(solution)/shard_map/ppermute | solution.py:315
  58.7 3.6 %collective-permute-start.4 = (bf16[256,1024]{1,0:T(8,128)(2,1)S(1)}, bf16[256,1024]{1,0:T(8,128)(2,1)}, u32[]{:S(2)}, u32[]{:S(2)}) collective-permute-start(bf16[256,1024]{1,0:T(8,128)(2,1)S(1)} %pad_maximum_fusion.refs_0_), channel_id=1, source_target_pairs={{0,24},{1,25},{2,26},{3,27},{4,28},{5,29},{6,30},{7,31},{8,0},{9,1... | collective-permute-start | bytes 1572872 | tf_op jit(solution)/shard_map/ppermute | solution.py:313
  62.3 1.9 %collective-permute-start.5 = (bf16[256,1024]{1,0:T(8,128)(2,1)S(1)}, bf16[256,1024]{1,0:T(8,128)(2,1)}, u32[]{:S(2)}, u32[]{:S(2)}) collective-permute-start(bf16[256,1024]{1,0:T(8,128)(2,1)S(1)} %constant_dynamic-update-slice_fusion.refs_1_), channel_id=1, source_target_pairs={{0,8},{1,9},{2,10},{3,11},{4,12},{5,13},{6,14},{7,15},{8,16},{9,17... | collective-permute-start | bytes 1572872 | tf_op jit(solution)/shard_map/ppermute | solution.py:316
  64.7 1.9 %collective-permute-start.7 = (bf16[256,1024]{1,0:T(8,128)(2,1)S(1)}, bf16[256,1024]{1,0:T(8,128)(2,1)}, u32[]{:S(2)}, u32[]{:S(2)}) collective-permute-start(bf16[256,1024]{1,0:T(8,128)(2,1)S(1)} %collective-permute-done.3.refs_2_), channel_id=1, source_target_pairs={{0,8},{1,9},{2,10},{3,11},{4,12},{5,13},{6,14},{7,15},{8,16},{9,17... | collective-permute-start | bytes 1572872 | tf_op jit(solution)/shard_map/ppermute | solution.py:317
  66.6 4.6 %collective-permute-start.8 = (bf16[256,1024]{1,0:T(8,128)(2,1)S(1)}, bf16[256,1024]{1,0:T(8,128)(2,1)}, u32[]{:S(2)}, u32[]{:S(2)}) collective-permute-start(bf16[256,1024]{1,0:T(8,128)(2,1)S(1)} %collective-permute-done.6.refs_5_), channel_id=1, source_target_pairs={{0,24},{1,25},{2,26},{3,27},{4,28},{5,29},{6,30},{7,31},{8,0},{9,1... | collective-permute-start | bytes 1572872 | tf_op jit(solution)/shard_map/ppermute | solution.py:318
  71.2 10.7 %collective-permute-start.12 = (bf16[16,104,128]{2,1,0:T(8,128)(2,1)S(1)}, bf16[16,104,128]{2,1,0:T(8,128)(2,1)S(1)}, u32[]{:S(2)}, u32[]{:S(2)}) collective-permute-start(bf16[16,104,128]{2,1,0:T(8,128)(2,1)S(1)} %all-to-all-done.1.mine_ref), channel_id=1, source_target_pairs={{0,32},{32,0},{1,33},{33,1},{2,34},{34,2},{3,35},{35,3},{4,36},{36... | collective-permute-start | bytes 1277960 | tf_op jit(solution)/shard_map/ppermute | solution.py:304
  82.0 1.8 %shard_map.69 = (f32[16,240,128]{2,1,0:T(8,128)S(1)}, f32[2,16,128]{2,1,0:T(8,128)S(1)}) custom-call(bf16[16,104,128]{2,1,0:T(8,128)(2,1)S(1)} %all-to-all-done.1.mine_ref), custom_call_target="tpu_custom_call" | custom-call | tf_op jit(solution)/shard_map/pallas_call | solution.py:255
  84.0 4.7 %shard_map.70.refs_11_ = bf16[200,1024]{1,0:T(8,128)(2,1)S(1)} custom-call(bf16[256,1024]{1,0:T(8,128)(2,1)S(1)} %pad_maximum_fusion.refs_0_, bf16[256,1024]{1,0:T(8,128)(2,1)S(1)} %constant_dynamic-update-slice_fusion.refs_1_, bf16[256,1024]{1,0:T(8,128)(2,1)S(1)} %collective-permute-done.3.refs_2_, bf16[256,1024]{1,0:T(8,128)(2,1)} %collective-permute-done.4.refs_3_, ...), custom_call_target="tpu_custom_call" | custom-call | tf_op jit(solution)/shard_map/pallas_call | solution.py:255
  88.8 7.0 %collective-permute-start.13 = (bf16[200,1024]{1,0:T(8,128)(2,1)S(1)}, bf16[200,1024]{1,0:T(8,128)(2,1)S(1)}, u32[]{:S(2)}, u32[]{:S(2)}) collective-permute-start(bf16[200,1024]{1,0:T(8,128)(2,1)S(1)} %shard_map.70.refs_11_), channel_id=1, source_target_pairs={{0,32},{32,0},{1,33},{33,1},{2,34},{34,2},{3,35},{35,3},{4,36},{36... | collective-permute-start | bytes 1228808 | tf_op jit(solution)/shard_map/ppermute | solution.py:331
  95.7 1.4 %collective-permute-done.13.refs_12_ = bf16[200,1024]{1,0:T(8,128)(2,1)S(1)} collective-permute-done((bf16[200,1024]{1,0:T(8,128)(2,1)S(1)}, bf16[200,1024]{1,0:T(8,128)(2,1)S(1)}, u32[]{:S(2)}, u32[]{:S(2)}) %collective-permute-start.13) | collective-permute-done | bytes 409632 | tf_op jit(solution)/shard_map/ppermute | solution.py:331
  97.1 4.8 %shard_map.71 = (f32[8,64,128]{2,1,0:T(8,128)S(1)}, bf16[8,64,128]{2,1,0:T(8,128)(2,1)S(1)}) custom-call(bf16[256,1024]{1,0:T(8,128)(2,1)S(1)} %pad_maximum_fusion.refs_0_, bf16[256,1024]{1,0:T(8,128)(2,1)S(1)} %constant_dynamic-update-slice_fusion.refs_1_, bf16[256,1024]{1,0:T(8,128)(2,1)S(1)} %collective-permute-done.3.refs_2_, ...), custom_call_target="tpu_custom_call" | custom-call | tf_op jit(solution)/shard_map/pallas_call | solution.py:255
  101.9 2.3 %collective-permute-start.14 = (bf16[8,64,128]{2,1,0:T(8,128)(2,1)S(1)}, bf16[8,64,128]{2,1,0:T(8,128)(2,1)S(1)}, u32[]{:S(2)}, u32[]{:S(2)}) collective-permute-start(bf16[8,64,128]{2,1,0:T(8,128)(2,1)S(1)} %get-tuple-element.18), channel_id=1, source_target_pairs={{0,32},{32,0},{1,33},{33,1},{2,34},{34,2},{3,35},{35,3},{4,36},{36... | collective-permute-start | bytes 393224 | tf_op jit(solution)/shard_map/ppermute | solution.py:335
  104.2 1.0 collective-permute-done.14.got_ref
  105.2 19.4 %all_to_all.15.back_ref = bf16[8,64,128]{2,1,0:T(8,128)(2,1)S(1)} all-to-all(bf16[8,64,128]{2,1,0:T(8,128)(2,1)S(1)} %shard_map.72), channel_id=1, replica_groups=mesh['zl'=8,'core'=2,'y'=4,'zh'=2,'x'=4] {'zl'}, dimensions={0} | all-to-all | bytes 262144 | tf_op jit(solution)/shard_map/all_to_all | solution.py:337
  124.6 0.8 shard_map.73
  (34 shorter events, 1.3 us)
Async XLA Ops:
  0.0 1.0 copy-start
  0.0 26.2 %copy-start.5 = (f32[256]{0:T(256)S(1)}, f32[256]{0:T(256)}, u32[]{:S(2)}) copy-start(f32[256]{0:T(256)} %param.11) | copy-start | bytes 3076
  0.0 26.2 %copy-start.4 = (f32[256,8]{0,1:T(8,128)S(1)}, f32[256,8]{0,1:T(8,128)}, u32[]{:S(2)}) copy-start(f32[256,8]{0,1:T(8,128)} %param.9) | copy-start | bytes 24580
  0.0 26.2 %copy-start.6 = (f32[256]{0:T(256)S(1)}, f32[256]{0:T(256)}, u32[]{:S(2)}) copy-start(f32[256]{0:T(256)} %param.8) | copy-start | bytes 3076
  1.8 29.3 %all-to-all-start = ((bf16[8,16,1024]{2,1,0:T(8,128)(2,1)}), bf16[8,16,1024]{2,1,0:T(8,128)(2,1)S(1)}, u32[]{:S(2)}, u32[]{:S(2)}) async-start(bf16[8,16,1024]{2,1,0:T(8,128)(2,1)} %broadcast_in_dim.12), calls=%async_computation | async-start | bytes 524288 | tf_op jit(solution)/shard_map/all_to_all | solution.py:270
  14.8 0.9 copy-start.1
  15.7 0.8 copy-start.3
  16.6 5.0 %collective-permute-start.9 = (bf16[160,128]{1,0:T(8,128)(2,1)S(1)}, bf16[160,128]{1,0:T(8,128)(2,1)S(1)}, u32[]{:S(2)}, u32[]{:S(2)}) collective-permute-start(bf16[160,128]{1,0:T(8,128)(2,1)S(1)} %shard_map.65), channel_id=1, source_target_pairs={{4,12},{5,13},{6,14},{7,15},{8,0},{9,1},{10,2},{11,3},{12,20},{13,... | collective-permute-start | bytes 122888 | tf_op jit(solution)/shard_map/ppermute | solution.py:279
  21.7 4.5 %collective-permute-start.10 = (bf16[80,128]{1,0:T(8,128)(2,1)S(1)}, bf16[80,128]{1,0:T(8,128)(2,1)S(1)}, u32[]{:S(2)}, u32[]{:S(2)}) collective-permute-start(bf16[80,128]{1,0:T(8,128)(2,1)S(1)} %get-tuple-element.13), channel_id=1, source_target_pairs={{0,1},{1,2},{2,3},{4,5},{5,6},{6,7},{8,9},{9,10},{10,11},{12,13},{... | collective-permute-start | bytes 61448 | tf_op jit(solution)/shard_map/ppermute | solution.py:290
  24.9 4.8 %collective-permute-start.11 = (bf16[80,128]{1,0:T(8,128)(2,1)S(1)}, bf16[80,128]{1,0:T(8,128)(2,1)S(1)}, u32[]{:S(2)}, u32[]{:S(2)}) collective-permute-start(bf16[80,128]{1,0:T(8,128)(2,1)S(1)} %get-tuple-element.14), channel_id=1, source_target_pairs={{1,0},{2,1},{3,2},{5,4},{6,5},{7,6},{9,8},{10,9},{11,10},{13,12},{... | collective-permute-start | bytes 61448 | tf_op jit(solution)/shard_map/ppermute | solution.py:291
  31.1 40.1 %all-to-all-start.1 = ((bf16[16,104,128]{2,1,0:T(8,128)(2,1)}), bf16[16,104,128]{2,1,0:T(8,128)(2,1)S(1)}, u32[]{:S(2)}, u32[]{:S(2)}) async-start(bf16[16,104,128]{2,1,0:T(8,128)(2,1)} %shard_map.67), calls=%async_computation.1 | async-start | bytes 851968 | tf_op jit(solution)/shard_map/all_to_all | solution.py:303
  40.3 10.1 %collective-permute-start = (bf16[128,1024]{1,0:T(8,128)(2,1)S(1)}, bf16[128,1024]{1,0:T(8,128)(2,1)S(1)}, u32[]{:S(2)}, u32[]{:S(2)}) collective-permute-start(bf16[128,1024]{1,0:T(8,128)(2,1)S(1)} %bitcast.12), channel_id=1, source_target_pairs={{0,1},{1,2},{2,3},{3,0},{4,5},{5,6},{6,7},{7,4},{8,9},{9,10},{10,1... | collective-permute-start | bytes 786440 | tf_op jit(solution)/shard_map/ppermute | solution.py:307
  43.5 10.1 %collective-permute-start.1 = (bf16[128,1024]{1,0:T(8,128)(2,1)S(1)}, bf16[128,1024]{1,0:T(8,128)(2,1)S(1)}, u32[]{:S(2)}, u32[]{:S(2)}) collective-permute-start(bf16[128,1024]{1,0:T(8,128)(2,1)S(1)} %bitcast.13), channel_id=1, source_target_pairs={{0,3},{1,0},{2,1},{3,2},{4,7},{5,4},{6,5},{7,6},{8,11},{9,8},{10,9... | collective-permute-start | bytes 786440 | tf_op jit(solution)/shard_map/ppermute | solution.py:308
  46.8 8.9 %collective-permute-start.2 = (bf16[128,1024]{1,0:T(8,128)(2,1)S(1)}, bf16[128,1024]{1,0:T(8,128)(2,1)S(1)}, u32[]{:S(2)}, u32[]{:S(2)}) collective-permute-start(bf16[128,1024]{1,0:T(8,128)(2,1)S(1)} %bitcast.14), channel_id=1, source_target_pairs={{0,2},{1,3},{2,0},{3,1},{4,6},{5,7},{6,4},{7,5},{8,10},{9,11},{10,... | collective-permute-start | bytes 786440 | tf_op jit(solution)/shard_map/ppermute | solution.py:310
  50.5 14.2 %collective-permute-start.3 = (bf16[256,1024]{1,0:T(8,128)(2,1)S(1)}, bf16[256,1024]{1,0:T(8,128)(2,1)S(1)}, u32[]{:S(2)}, u32[]{:S(2)}) collective-permute-start(bf16[256,1024]{1,0:T(8,128)(2,1)S(1)} %pad_maximum_fusion.refs_0_), channel_id=1, source_target_pairs={{0,8},{1,9},{2,10},{3,11},{4,12},{5,13},{6,14},{7,15},{8,16},{9,17... | collective-permute-start | bytes 1572872 | tf_op jit(solution)/shard_map/ppermute | solution.py:312
  55.7 10.9 %collective-permute-start.6 = (bf16[256,1024]{1,0:T(8,128)(2,1)S(1)}, bf16[256,1024]{1,0:T(8,128)(2,1)S(1)}, u32[]{:S(2)}, u32[]{:S(2)}) collective-permute-start(bf16[256,1024]{1,0:T(8,128)(2,1)S(1)} %constant_dynamic-update-slice_fusion.refs_1_), channel_id=1, source_target_pairs={{0,24},{1,25},{2,26},{3,27},{4,28},{5,29},{6,30},{7,31},{8,0},{9,1... | collective-permute-start | bytes 1572872 | tf_op jit(solution)/shard_map/ppermute | solution.py:315
  58.7 25.3 %collective-permute-start.4 = (bf16[256,1024]{1,0:T(8,128)(2,1)S(1)}, bf16[256,1024]{1,0:T(8,128)(2,1)}, u32[]{:S(2)}, u32[]{:S(2)}) collective-permute-start(bf16[256,1024]{1,0:T(8,128)(2,1)S(1)} %pad_maximum_fusion.refs_0_), channel_id=1, source_target_pairs={{0,24},{1,25},{2,26},{3,27},{4,28},{5,29},{6,30},{7,31},{8,0},{9,1... | collective-permute-start | bytes 1572872 | tf_op jit(solution)/shard_map/ppermute | solution.py:313
  62.3 21.7 %collective-permute-start.5 = (bf16[256,1024]{1,0:T(8,128)(2,1)S(1)}, bf16[256,1024]{1,0:T(8,128)(2,1)}, u32[]{:S(2)}, u32[]{:S(2)}) collective-permute-start(bf16[256,1024]{1,0:T(8,128)(2,1)S(1)} %constant_dynamic-update-slice_fusion.refs_1_), channel_id=1, source_target_pairs={{0,8},{1,9},{2,10},{3,11},{4,12},{5,13},{6,14},{7,15},{8,16},{9,17... | collective-permute-start | bytes 1572872 | tf_op jit(solution)/shard_map/ppermute | solution.py:316
  64.7 19.3 %collective-permute-start.7 = (bf16[256,1024]{1,0:T(8,128)(2,1)S(1)}, bf16[256,1024]{1,0:T(8,128)(2,1)}, u32[]{:S(2)}, u32[]{:S(2)}) collective-permute-start(bf16[256,1024]{1,0:T(8,128)(2,1)S(1)} %collective-permute-done.3.refs_2_), channel_id=1, source_target_pairs={{0,8},{1,9},{2,10},{3,11},{4,12},{5,13},{6,14},{7,15},{8,16},{9,17... | collective-permute-start | bytes 1572872 | tf_op jit(solution)/shard_map/ppermute | solution.py:317
  66.6 17.4 %collective-permute-start.8 = (bf16[256,1024]{1,0:T(8,128)(2,1)S(1)}, bf16[256,1024]{1,0:T(8,128)(2,1)}, u32[]{:S(2)}, u32[]{:S(2)}) collective-permute-start(bf16[256,1024]{1,0:T(8,128)(2,1)S(1)} %collective-permute-done.6.refs_5_), channel_id=1, source_target_pairs={{0,24},{1,25},{2,26},{3,27},{4,28},{5,29},{6,30},{7,31},{8,0},{9,1... | collective-permute-start | bytes 1572872 | tf_op jit(solution)/shard_map/ppermute | solution.py:318
  71.2 12.5 %collective-permute-start.12 = (bf16[16,104,128]{2,1,0:T(8,128)(2,1)S(1)}, bf16[16,104,128]{2,1,0:T(8,128)(2,1)S(1)}, u32[]{:S(2)}, u32[]{:S(2)}) collective-permute-start(bf16[16,104,128]{2,1,0:T(8,128)(2,1)S(1)} %all-to-all-done.1.mine_ref), channel_id=1, source_target_pairs={{0,32},{32,0},{1,33},{33,1},{2,34},{34,2},{3,35},{35,3},{4,36},{36... | collective-permute-start | bytes 1277960 | tf_op jit(solution)/shard_map/ppermute | solution.py:304
  88.7 35.8 %copy-start.2 = (bf16[64,8,128]{2,1,0:T(8,128)(2,1)S(1)}, bf16[64,8,128]{2,1,0:T(8,128)(2,1)}, u32[]{:S(2)}) copy-start(bf16[64,8,128]{2,1,0:T(8,128)(2,1)} %param.6) | copy-start | bytes 393220
  88.8 8.3 %collective-permute-start.13 = (bf16[200,1024]{1,0:T(8,128)(2,1)S(1)}, bf16[200,1024]{1,0:T(8,128)(2,1)S(1)}, u32[]{:S(2)}, u32[]{:S(2)}) collective-permute-start(bf16[200,1024]{1,0:T(8,128)(2,1)S(1)} %shard_map.70.refs_11_), channel_id=1, source_target_pairs={{0,32},{32,0},{1,33},{33,1},{2,34},{34,2},{3,35},{35,3},{4,36},{36... | collective-permute-start | bytes 1228808 | tf_op jit(solution)/shard_map/ppermute | solution.py:331
  101.9 3.3 %collective-permute-start.14 = (bf16[8,64,128]{2,1,0:T(8,128)(2,1)S(1)}, bf16[8,64,128]{2,1,0:T(8,128)(2,1)S(1)}, u32[]{:S(2)}, u32[]{:S(2)}) collective-permute-start(bf16[8,64,128]{2,1,0:T(8,128)(2,1)S(1)} %get-tuple-element.18), channel_id=1, source_target_pairs={{0,32},{32,0},{1,33},{33,1},{2,34},{34,2},{3,35},{35,3},{4,36},{36... | collective-permute-start | bytes 393224 | tf_op jit(solution)/shard_map/ppermute | solution.py:335

commit v2 on v1

--- a/solution.py
+++ b/solution.py
@@ -15,6 +15,7 @@
 VM = pltpu.VMEM
 OFFS = (0, -1, 1, 2)
 ARRIVAL = tuple((o, i) for o, half in ((0, 0), (0, 2), (1, 0), (2, 0), (1, 2), (2, 2), (3, 0), (3, 2)) for i in (half, half + 1))
+CHIPS = (0, 4, 2, 6, 1, 5, 3, 7)
 ALL = ("zl", "core", "y", "zh", "x")
 SPLIT = (8, 2, 4, 2, 4)
 
@@ -120,8 +121,9 @@
 
 def coef_kernel(mine_ref, coef_ref, wr_ref, scr_ref, par_ref, log_ref):
     core, y, zh, x = (lax.axis_index(axis) for axis in ("core", "y", "zh", "x"))
+    zl = lax.axis_index("zl")
     for z in range(8):
-        scr_ref[z * 40 : (z + 1) * 40, :] = mine_ref[8 - 8 * zh + z].astype(F32)[56:96]
+        scr_ref[z * 40 : (z + 1) * 40, :] = mine_ref[8 - 8 * zh + (zl ^ CHIPS[z])].astype(F32)[56:96]
     sub = lax.broadcasted_iota(jnp.int32, (8, 128), 0)
     grp = lax.broadcasted_iota(jnp.int32, (8, 128), 1) // 16
     for v in range(10):
@@ -266,8 +268,10 @@
     y, x = lax.axis_index("y"), lax.axis_index("x")
 
     part = lax.dynamic_slice_in_dim(basis_rows, (y * 4 + x) * 16, 16, axis=0)
-    send = jnp.broadcast_to(part[None], (8, 16, 1024))
-    shard = lax.all_to_all(send, "zl", 0, 0, tiled=True).reshape(128, 1024)
+    shard = part
+    for hop in (4, 2, 1):
+        got = lax.ppermute(shard, "zl", [(i, i ^ hop) for i in range(8)])
+        shard = jnp.concatenate([shard, got], axis=0)
 
     modes, logs = modes_now.reshape(512, 128), log_fields.reshape(64, 128)
     scratch = [VM((512, 128), F32), VM((64, 128), F32)]

time: 127 us -> 144 us (1.13)
  waiting for transfers between devices: 11.9 us -> 25.4 us
  starting transfers between devices: 76.1 us -> 81.1 us
    ppermute x0 -> x3, waiting for transfers between devices: none -> 18 us  [update(): got = lax.ppermute(shard, 'zl', [(i, i ^ hop) for i in range(8)])]
    ppermute x0 -> x3, starting transfers between devices: none -> 17.8 us  [update(): got = lax.ppermute(shard, 'zl', [(i, i ^ hop) for i in range(8)])]
    all_to_all x1 -> x0, starting transfers between devices: 13.1 us -> none  [update(): shard = lax.all_to_all(send, 'zl', 0, 0, tiled=True).reshape(128, 1024)]
    ppermute x1, waiting for transfers between devices: 3.52 us -> 0.01 us  [update(): got = lax.ppermute(rows, ALL, shift(toward))]
  transfers between devices with their start and end apart: 17 -> 19, of which waited for: 6 -> 6; matrix products, arithmetic and copies ran while one was open for 0% -> 1% of each run, Pallas kernels for 3% -> 3%
where the time goes in v2:
time: 144 us; the launch traced here: 143 us
  starting transfers between devices  81.1 us (56%)
  waiting for transfers between devices  25.4 us (18%)
  blocking collectives  18.5 us (13%)
  Pallas kernels  13.9 us (10%)
  local copies, waits for them, and re-layouts  2.51 us (2%)
    all_to_all x1, blocking collectives, update(): back = lax.all_to_all(out, 'zl', 0, 0, tiled=True)  18.5 us
    ppermute x3, waiting for transfers between devices, update(): got = lax.ppermute(shard, 'zl', [(i, i ^ hop) for i in range(8)])  18 us
    ppermute x3, starting transfers between devices, update(): got = lax.ppermute(shard, 'zl', [(i, i ^ hop) for i in range(8)])  17.8 us
    pallas_call x10, Pallas kernels, call(): pl.pallas_call(kernel, out_shape=outs, in_specs=specs, out_specs=WHOLE if...  13.9 us
    ppermute x1, starting transfers between devices, update(): theirs = lax.ppermute(mine, 'core', [(0, 1), (1, 0)])  11 us
    all_to_all x1, starting transfers between devices, update(): mine = lax.all_to_all(patch, ('zh', 'zl'), 0, 0, tiled=True)  10.2 us
    ppermute x1, starting transfers between devices, update(): other = lax.ppermute(own, 'core', [(0, 1), (1, 0)])  6.18 us
    ppermute x1, starting transfers between devices, update(): away_far = lax.ppermute(away_more, ALL, bwd)  4.57 us
  transfers between devices with their start and end apart: 19, of which 6 were waited for; matrix products, arithmetic and copies ran while one was open for 1% of the time, Pallas kernels for 3%

profile of v2, /device:TPU:1, one launch (start us, length us, event | category | flops | bytes accessed | tf_op | source)
XLA Modules:
  0.0 142.6 jit_solution(30463687881990576)
XLA Ops:
  0.0 0.8 constant_dynamic-update-slice_fusion.4
  0.8 9.6 %collective-permute-start = (bf16[16,1024]{1,0:T(8,128)(2,1)S(1)}, bf16[16,1024]{1,0:T(8,128)(2,1)S(1)}, u32[]{:S(2)}, u32[]{:S(2)}) collective-permute-start(bf16[16,1024]{1,0:T(8,128)(2,1)S(1)} %get-tuple-element.20), channel_id=1, source_target_pairs={{0,256},{64,320},{128,384},{192,448},{256,0},{320,64},{384,128},{4... | collective-permute-start | bytes 98312 | tf_op jit(solution)/shard_map/ppermute | solution.py:273
  10.4 0.9 copy-done
  12.1 1.3 collective-permute-start.12
  13.7 4.9 %collective-permute-start.1 = (bf16[32,1024]{1,0:T(8,128)(2,1)S(1)}, bf16[32,1024]{1,0:T(8,128)(2,1)S(1)}, u32[]{:S(2)}, u32[]{:S(2)}) collective-permute-start(bf16[32,1024]{1,0:T(8,128)(2,1)S(1)} %pad_maximum_fusion.2), channel_id=1, source_target_pairs={{0,128},{64,192},{128,0},{192,64},{256,384},{320,448},{384,256},{4... | collective-permute-start | bytes 196616 | tf_op jit(solution)/shard_map/ppermute | solution.py:273
  18.7 3.1 %collective-permute-start.13 = (bf16[80,128]{1,0:T(8,128)(2,1)S(1)}, bf16[80,128]{1,0:T(8,128)(2,1)S(1)}, u32[]{:S(2)}, u32[]{:S(2)}) collective-permute-start(bf16[80,128]{1,0:T(8,128)(2,1)S(1)} %get-tuple-element.13), channel_id=1, source_target_pairs={{0,1},{1,2},{2,3},{4,5},{5,6},{6,7},{8,9},{9,10},{10,11},{12,13},{... | collective-permute-start | bytes 61448 | tf_op jit(solution)/shard_map/ppermute | solution.py:294
  21.8 1.3 collective-permute-start.14
  23.9 2.5 %collective-permute-done.14.right_ref = bf16[80,128]{1,0:T(8,128)(2,1)S(1)} collective-permute-done((bf16[80,128]{1,0:T(8,128)(2,1)S(1)}, bf16[80,128]{1,0:T(8,128)(2,1)S(1)}, u32[]{:S(2)}, u32[]{:S(2)}) %collective-permute-start.14) | collective-permute-done | bytes 20512 | tf_op jit(solution)/shard_map/ppermute | solution.py:295
  26.4 1.5 %shard_map.67 = bf16[16,104,128]{2,1,0:T(8,128)(2,1)} custom-call(f32[10,144,128]{2,1,0:T(8,128)S(1)} %get-tuple-element.12.full_ref, bf16[80,128]{1,0:T(8,128)(2,1)S(1)} %collective-permute-done.13.left_ref, bf16[80,128]{1,0:T(8,128)(2,1)S(1)} %collective-permute-done.14.right_ref, f32[20,128]{1,0:T(8,128)S(1)} %reshape.14.pars_ref), custom_call_target="tpu_custom_call" | custom-call | tf_op jit(solution)/shard_map/pallas_call | solution.py:257
  27.8 10.2 %all-to-all-start = ((bf16[16,104,128]{2,1,0:T(8,128)(2,1)}), bf16[16,104,128]{2,1,0:T(8,128)(2,1)S(1)}, u32[]{:S(2)}, u32[]{:S(2)}) async-start(bf16[16,104,128]{2,1,0:T(8,128)(2,1)} %shard_map.67), calls=%async_computation | async-start | bytes 851968 | tf_op jit(solution)/shard_map/all_to_all | solution.py:307
  38.1 3.3 %collective-permute-start.2 = (bf16[64,1024]{1,0:T(8,128)(2,1)S(1)}, bf16[64,1024]{1,0:T(8,128)(2,1)S(1)}, u32[]{:S(2)}, u32[]{:S(2)}) collective-permute-start(bf16[64,1024]{1,0:T(8,128)(2,1)S(1)} %pad_maximum_fusion.1), channel_id=1, source_target_pairs={{0,64},{64,0},{128,192},{192,128},{256,320},{320,256},{384,448},{4... | collective-permute-start | bytes 393224 | tf_op jit(solution)/shard_map/ppermute | solution.py:273
  41.4 18.0 %collective-permute-done.2 = bf16[64,1024]{1,0:T(8,128)(2,1)S(1)} collective-permute-done((bf16[64,1024]{1,0:T(8,128)(2,1)S(1)}, bf16[64,1024]{1,0:T(8,128)(2,1)S(1)}, u32[]{:S(2)}, u32[]{:S(2)}) %collective-permute-start.2) | collective-permute-done | bytes 131104 | tf_op jit(solution)/shard_map/ppermute | solution.py:273
  59.4 3.2 %collective-permute-start.3 = (bf16[128,1024]{1,0:T(8,128)(2,1)S(1)}, bf16[128,1024]{1,0:T(8,128)(2,1)S(1)}, u32[]{:S(2)}, u32[]{:S(2)}) collective-permute-start(bf16[128,1024]{1,0:T(8,128)(2,1)S(1)} %pad_maximum_fusion), channel_id=1, source_target_pairs={{0,1},{1,2},{2,3},{3,0},{4,5},{5,6},{6,7},{7,4},{8,9},{9,10},{10,1... | collective-permute-start | bytes 786440 | tf_op jit(solution)/shard_map/ppermute | solution.py:311
  62.6 3.3 %collective-permute-start.4 = (bf16[128,1024]{1,0:T(8,128)(2,1)S(1)}, bf16[128,1024]{1,0:T(8,128)(2,1)S(1)}, u32[]{:S(2)}, u32[]{:S(2)}) collective-permute-start(bf16[128,1024]{1,0:T(8,128)(2,1)S(1)} %pad_maximum_fusion), channel_id=1, source_target_pairs={{0,3},{1,0},{2,1},{3,2},{4,7},{5,4},{6,5},{7,6},{8,11},{9,8},{10,9... | collective-permute-start | bytes 786440 | tf_op jit(solution)/shard_map/ppermute | solution.py:312
  65.9 3.3 %collective-permute-start.5 = (bf16[128,1024]{1,0:T(8,128)(2,1)S(1)}, bf16[128,1024]{1,0:T(8,128)(2,1)S(1)}, u32[]{:S(2)}, u32[]{:S(2)}) collective-permute-start(bf16[128,1024]{1,0:T(8,128)(2,1)S(1)} %pad_maximum_fusion), channel_id=1, source_target_pairs={{0,2},{1,3},{2,0},{3,1},{4,6},{5,7},{6,4},{7,5},{8,10},{9,11},{10,... | collective-permute-start | bytes 786440 | tf_op jit(solution)/shard_map/ppermute | solution.py:314
  69.3 3.1 %collective-permute-start.6 = (bf16[256,1024]{1,0:T(8,128)(2,1)S(1)}, bf16[256,1024]{1,0:T(8,128)(2,1)S(1)}, u32[]{:S(2)}, u32[]{:S(2)}) collective-permute-start(bf16[256,1024]{1,0:T(8,128)(2,1)S(1)} %constant_dynamic-update-slice_fusion.refs_0_), channel_id=1, source_target_pairs={{0,8},{1,9},{2,10},{3,11},{4,12},{5,13},{6,14},{7,15},{8,16},{9,17... | collective-permute-start | bytes 1572872 | tf_op jit(solution)/shard_map/ppermute | solution.py:316
  72.5 2.0 %collective-permute-done.5 = bf16[128,1024]{1,0:T(8,128)(2,1)S(1)} collective-permute-done((bf16[128,1024]{1,0:T(8,128)(2,1)S(1)}, bf16[128,1024]{1,0:T(8,128)(2,1)S(1)}, u32[]{:S(2)}, u32[]{:S(2)}) %collective-permute-start.5) | collective-permute-done | bytes 262176 | tf_op jit(solution)/shard_map/ppermute | solution.py:314
  74.6 2.9 %collective-permute-start.9 = (bf16[256,1024]{1,0:T(8,128)(2,1)S(1)}, bf16[256,1024]{1,0:T(8,128)(2,1)S(1)}, u32[]{:S(2)}, u32[]{:S(2)}) collective-permute-start(bf16[256,1024]{1,0:T(8,128)(2,1)S(1)} %constant_dynamic-update-slice_fusion.5.refs_1_), channel_id=1, source_target_pairs={{0,24},{1,25},{2,26},{3,27},{4,28},{5,29},{6,30},{7,31},{8,0},{9,1... | collective-permute-start | bytes 1572872 | tf_op jit(solution)/shard_map/ppermute | solution.py:319
  77.5 3.6 %collective-permute-start.7 = (bf16[256,1024]{1,0:T(8,128)(2,1)S(1)}, bf16[256,1024]{1,0:T(8,128)(2,1)S(1)}, u32[]{:S(2)}, u32[]{:S(2)}) collective-permute-start(bf16[256,1024]{1,0:T(8,128)(2,1)S(1)} %constant_dynamic-update-slice_fusion.refs_0_), channel_id=1, source_target_pairs={{0,24},{1,25},{2,26},{3,27},{4,28},{5,29},{6,30},{7,31},{8,0},{9,1... | collective-permute-start | bytes 1572872 | tf_op jit(solution)/shard_map/ppermute | solution.py:317
  81.1 1.9 %collective-permute-start.8 = (bf16[256,1024]{1,0:T(8,128)(2,1)S(1)}, bf16[256,1024]{1,0:T(8,128)(2,1)}, u32[]{:S(2)}, u32[]{:S(2)}) collective-permute-start(bf16[256,1024]{1,0:T(8,128)(2,1)S(1)} %constant_dynamic-update-slice_fusion.5.refs_1_), channel_id=1, source_target_pairs={{0,8},{1,9},{2,10},{3,11},{4,12},{5,13},{6,14},{7,15},{8,16},{9,17... | collective-permute-start | bytes 1572872 | tf_op jit(solution)/shard_map/ppermute | solution.py:320
  83.6 1.9 %collective-permute-start.10 = (bf16[256,1024]{1,0:T(8,128)(2,1)S(1)}, bf16[256,1024]{1,0:T(8,128)(2,1)}, u32[]{:S(2)}, u32[]{:S(2)}) collective-permute-start(bf16[256,1024]{1,0:T(8,128)(2,1)S(1)} %collective-permute-done.6.refs_2_), channel_id=1, source_target_pairs={{0,8},{1,9},{2,10},{3,11},{4,12},{5,13},{6,14},{7,15},{8,16},{9,17... | collective-permute-start | bytes 1572872 | tf_op jit(solution)/shard_map/ppermute | solution.py:321
  85.5 4.6 %collective-permute-start.11 = (bf16[256,1024]{1,0:T(8,128)(2,1)S(1)}, bf16[256,1024]{1,0:T(8,128)(2,1)}, u32[]{:S(2)}, u32[]{:S(2)}) collective-permute-start(bf16[256,1024]{1,0:T(8,128)(2,1)S(1)} %collective-permute-done.9.refs_5_), channel_id=1, source_target_pairs={{0,24},{1,25},{2,26},{3,27},{4,28},{5,29},{6,30},{7,31},{8,0},{9,1... | collective-permute-start | bytes 1572872 | tf_op jit(solution)/shard_map/ppermute | solution.py:322
  90.1 11.0 %collective-permute-start.15 = (bf16[16,104,128]{2,1,0:T(8,128)(2,1)S(1)}, bf16[16,104,128]{2,1,0:T(8,128)(2,1)S(1)}, u32[]{:S(2)}, u32[]{:S(2)}) collective-permute-start(bf16[16,104,128]{2,1,0:T(8,128)(2,1)S(1)} %all-to-all-done.mine_ref), channel_id=1, source_target_pairs={{0,32},{32,0},{1,33},{33,1},{2,34},{34,2},{3,35},{35,3},{4,36},{36... | collective-permute-start | bytes 1277960 | tf_op jit(solution)/shard_map/ppermute | solution.py:308
  101.1 1.8 %shard_map.69 = (f32[16,240,128]{2,1,0:T(8,128)S(1)}, f32[2,16,128]{2,1,0:T(8,128)S(1)}) custom-call(bf16[16,104,128]{2,1,0:T(8,128)(2,1)S(1)} %all-to-all-done.mine_ref), custom_call_target="tpu_custom_call" | custom-call | tf_op jit(solution)/shard_map/pallas_call | solution.py:257
  103.2 4.5 %shard_map.70.refs_11_ = bf16[200,1024]{1,0:T(8,128)(2,1)S(1)} custom-call(bf16[256,1024]{1,0:T(8,128)(2,1)S(1)} %constant_dynamic-update-slice_fusion.refs_0_, bf16[256,1024]{1,0:T(8,128)(2,1)S(1)} %constant_dynamic-update-slice_fusion.5.refs_1_, bf16[256,1024]{1,0:T(8,128)(2,1)S(1)} %collective-permute-done.6.refs_2_, ...), custom_call_target="tpu_custom_call" | custom-call | tf_op jit(solution)/shard_map/pallas_call | solution.py:257
  107.7 6.2 %collective-permute-start.16 = (bf16[200,1024]{1,0:T(8,128)(2,1)S(1)}, bf16[200,1024]{1,0:T(8,128)(2,1)S(1)}, u32[]{:S(2)}, u32[]{:S(2)}) collective-permute-start(bf16[200,1024]{1,0:T(8,128)(2,1)S(1)} %shard_map.70.refs_11_), channel_id=1, source_target_pairs={{0,32},{32,0},{1,33},{33,1},{2,34},{34,2},{3,35},{35,3},{4,36},{36... | collective-permute-start | bytes 1228808 | tf_op jit(solution)/shard_map/ppermute | solution.py:335
  113.9 1.4 collective-permute-done.16.refs_12_
  115.2 4.6 %shard_map.71 = (f32[8,64,128]{2,1,0:T(8,128)S(1)}, bf16[8,64,128]{2,1,0:T(8,128)(2,1)S(1)}) custom-call(bf16[256,1024]{1,0:T(8,128)(2,1)S(1)} %constant_dynamic-update-slice_fusion.refs_0_, bf16[256,1024]{1,0:T(8,128)(2,1)S(1)} %constant_dynamic-update-slice_fusion.5.refs_1_, bf16[256,1024]{1,0:T(8,128)(2,1)S(1)} %collective-permute-done.6.refs_2_, ...), custom_call_target="tpu_custom_call" | custom-call | tf_op jit(solution)/shard_map/pallas_call | solution.py:257
  119.9 2.3 %collective-permute-start.17 = (bf16[8,64,128]{2,1,0:T(8,128)(2,1)S(1)}, bf16[8,64,128]{2,1,0:T(8,128)(2,1)S(1)}, u32[]{:S(2)}, u32[]{:S(2)}) collective-permute-start(bf16[8,64,128]{2,1,0:T(8,128)(2,1)S(1)} %get-tuple-element.18), channel_id=1, source_target_pairs={{0,32},{32,0},{1,33},{33,1},{2,34},{34,2},{3,35},{35,3},{4,36},{36... | collective-permute-start | bytes 393224 | tf_op jit(solution)/shard_map/ppermute | solution.py:339
  122.2 1.0 collective-permute-done.17.got_ref
  123.2 18.5 %all_to_all.10.back_ref = bf16[8,64,128]{2,1,0:T(8,128)(2,1)S(1)} all-to-all(bf16[8,64,128]{2,1,0:T(8,128)(2,1)S(1)} %shard_map.72), channel_id=1, replica_groups=mesh['zl'=8,'core'=2,'y'=4,'zh'=2,'x'=4] {'zl'}, dimensions={0} | all-to-all | bytes 262144 | tf_op jit(solution)/shard_map/all_to_all | solution.py:341
  141.7 0.8 shard_map.73
  (35 shorter events, 2.8 us)
Async XLA Ops:
  0.8 12.9 %collective-permute-start = (bf16[16,1024]{1,0:T(8,128)(2,1)S(1)}, bf16[16,1024]{1,0:T(8,128)(2,1)S(1)}, u32[]{:S(2)}, u32[]{:S(2)}) collective-permute-start(bf16[16,1024]{1,0:T(8,128)(2,1)S(1)} %get-tuple-element.20), channel_id=1, source_target_pairs={{0,256},{64,320},{128,384},{192,448},{256,0},{320,64},{384,128},{4... | collective-permute-start | bytes 98312 | tf_op jit(solution)/shard_map/ppermute | solution.py:273
  10.4 0.9 copy-start
  11.3 0.8 copy-start.2
  12.1 6.5 %collective-permute-start.12 = (bf16[160,128]{1,0:T(8,128)(2,1)S(1)}, bf16[160,128]{1,0:T(8,128)(2,1)S(1)}, u32[]{:S(2)}, u32[]{:S(2)}) collective-permute-start(bf16[160,128]{1,0:T(8,128)(2,1)S(1)} %shard_map.65), channel_id=1, source_target_pairs={{4,12},{5,13},{6,14},{7,15},{8,0},{9,1},{10,2},{11,3},{12,20},{13,... | collective-permute-start | bytes 122888 | tf_op jit(solution)/shard_map/ppermute | solution.py:283
  13.7 24.4 %collective-permute-start.1 = (bf16[32,1024]{1,0:T(8,128)(2,1)S(1)}, bf16[32,1024]{1,0:T(8,128)(2,1)S(1)}, u32[]{:S(2)}, u32[]{:S(2)}) collective-permute-start(bf16[32,1024]{1,0:T(8,128)(2,1)S(1)} %pad_maximum_fusion.2), channel_id=1, source_target_pairs={{0,128},{64,192},{128,0},{192,64},{256,384},{320,448},{384,256},{4... | collective-permute-start | bytes 196616 | tf_op jit(solution)/shard_map/ppermute | solution.py:273
  18.7 5.2 %collective-permute-start.13 = (bf16[80,128]{1,0:T(8,128)(2,1)S(1)}, bf16[80,128]{1,0:T(8,128)(2,1)S(1)}, u32[]{:S(2)}, u32[]{:S(2)}) collective-permute-start(bf16[80,128]{1,0:T(8,128)(2,1)S(1)} %get-tuple-element.13), channel_id=1, source_target_pairs={{0,1},{1,2},{2,3},{4,5},{5,6},{6,7},{8,9},{9,10},{10,11},{12,13},{... | collective-permute-start | bytes 61448 | tf_op jit(solution)/shard_map/ppermute | solution.py:294
  21.8 4.5 %collective-permute-start.14 = (bf16[80,128]{1,0:T(8,128)(2,1)S(1)}, bf16[80,128]{1,0:T(8,128)(2,1)S(1)}, u32[]{:S(2)}, u32[]{:S(2)}) collective-permute-start(bf16[80,128]{1,0:T(8,128)(2,1)S(1)} %get-tuple-element.14), channel_id=1, source_target_pairs={{1,0},{2,1},{3,2},{5,4},{6,5},{7,6},{9,8},{10,9},{11,10},{13,12},{... | collective-permute-start | bytes 61448 | tf_op jit(solution)/shard_map/ppermute | solution.py:295
  27.8 62.3 %all-to-all-start = ((bf16[16,104,128]{2,1,0:T(8,128)(2,1)}), bf16[16,104,128]{2,1,0:T(8,128)(2,1)S(1)}, u32[]{:S(2)}, u32[]{:S(2)}) async-start(bf16[16,104,128]{2,1,0:T(8,128)(2,1)} %shard_map.67), calls=%async_computation | async-start | bytes 851968 | tf_op jit(solution)/shard_map/all_to_all | solution.py:307
  38.1 21.3 %collective-permute-start.2 = (bf16[64,1024]{1,0:T(8,128)(2,1)S(1)}, bf16[64,1024]{1,0:T(8,128)(2,1)S(1)}, u32[]{:S(2)}, u32[]{:S(2)}) collective-permute-start(bf16[64,1024]{1,0:T(8,128)(2,1)S(1)} %pad_maximum_fusion.1), channel_id=1, source_target_pairs={{0,64},{64,0},{128,192},{192,128},{256,320},{320,256},{384,448},{4... | collective-permute-start | bytes 393224 | tf_op jit(solution)/shard_map/ppermute | solution.py:273
  59.4 9.9 %collective-permute-start.3 = (bf16[128,1024]{1,0:T(8,128)(2,1)S(1)}, bf16[128,1024]{1,0:T(8,128)(2,1)S(1)}, u32[]{:S(2)}, u32[]{:S(2)}) collective-permute-start(bf16[128,1024]{1,0:T(8,128)(2,1)S(1)} %pad_maximum_fusion), channel_id=1, source_target_pairs={{0,1},{1,2},{2,3},{3,0},{4,5},{5,6},{6,7},{7,4},{8,9},{9,10},{10,1... | collective-permute-start | bytes 786440 | tf_op jit(solution)/shard_map/ppermute | solution.py:311
  62.6 9.9 %collective-permute-start.4 = (bf16[128,1024]{1,0:T(8,128)(2,1)S(1)}, bf16[128,1024]{1,0:T(8,128)(2,1)S(1)}, u32[]{:S(2)}, u32[]{:S(2)}) collective-permute-start(bf16[128,1024]{1,0:T(8,128)(2,1)S(1)} %pad_maximum_fusion), channel_id=1, source_target_pairs={{0,3},{1,0},{2,1},{3,2},{4,7},{5,4},{6,5},{7,6},{8,11},{9,8},{10,9... | collective-permute-start | bytes 786440 | tf_op jit(solution)/shard_map/ppermute | solution.py:312
  65.9 8.6 %collective-permute-start.5 = (bf16[128,1024]{1,0:T(8,128)(2,1)S(1)}, bf16[128,1024]{1,0:T(8,128)(2,1)S(1)}, u32[]{:S(2)}, u32[]{:S(2)}) collective-permute-start(bf16[128,1024]{1,0:T(8,128)(2,1)S(1)} %pad_maximum_fusion), channel_id=1, source_target_pairs={{0,2},{1,3},{2,0},{3,1},{4,6},{5,7},{6,4},{7,5},{8,10},{9,11},{10,... | collective-permute-start | bytes 786440 | tf_op jit(solution)/shard_map/ppermute | solution.py:314
  69.3 14.2 %collective-permute-start.6 = (bf16[256,1024]{1,0:T(8,128)(2,1)S(1)}, bf16[256,1024]{1,0:T(8,128)(2,1)S(1)}, u32[]{:S(2)}, u32[]{:S(2)}) collective-permute-start(bf16[256,1024]{1,0:T(8,128)(2,1)S(1)} %constant_dynamic-update-slice_fusion.refs_0_), channel_id=1, source_target_pairs={{0,8},{1,9},{2,10},{3,11},{4,12},{5,13},{6,14},{7,15},{8,16},{9,17... | collective-permute-start | bytes 1572872 | tf_op jit(solution)/shard_map/ppermute | solution.py:316
  74.6 10.9 %collective-permute-start.9 = (bf16[256,1024]{1,0:T(8,128)(2,1)S(1)}, bf16[256,1024]{1,0:T(8,128)(2,1)S(1)}, u32[]{:S(2)}, u32[]{:S(2)}) collective-permute-start(bf16[256,1024]{1,0:T(8,128)(2,1)S(1)} %constant_dynamic-update-slice_fusion.5.refs_1_), channel_id=1, source_target_pairs={{0,24},{1,25},{2,26},{3,27},{4,28},{5,29},{6,30},{7,31},{8,0},{9,1... | collective-permute-start | bytes 1572872 | tf_op jit(solution)/shard_map/ppermute | solution.py:319
  77.5 25.6 %collective-permute-start.7 = (bf16[256,1024]{1,0:T(8,128)(2,1)S(1)}, bf16[256,1024]{1,0:T(8,128)(2,1)S(1)}, u32[]{:S(2)}, u32[]{:S(2)}) collective-permute-start(bf16[256,1024]{1,0:T(8,128)(2,1)S(1)} %constant_dynamic-update-slice_fusion.refs_0_), channel_id=1, source_target_pairs={{0,24},{1,25},{2,26},{3,27},{4,28},{5,29},{6,30},{7,31},{8,0},{9,1... | collective-permute-start | bytes 1572872 | tf_op jit(solution)/shard_map/ppermute | solution.py:317
  81.1 22.0 %collective-permute-start.8 = (bf16[256,1024]{1,0:T(8,128)(2,1)S(1)}, bf16[256,1024]{1,0:T(8,128)(2,1)}, u32[]{:S(2)}, u32[]{:S(2)}) collective-permute-start(bf16[256,1024]{1,0:T(8,128)(2,1)S(1)} %constant_dynamic-update-slice_fusion.5.refs_1_), channel_id=1, source_target_pairs={{0,8},{1,9},{2,10},{3,11},{4,12},{5,13},{6,14},{7,15},{8,16},{9,17... | collective-permute-start | bytes 1572872 | tf_op jit(solution)/shard_map/ppermute | solution.py:320
  83.6 19.6 %collective-permute-start.10 = (bf16[256,1024]{1,0:T(8,128)(2,1)S(1)}, bf16[256,1024]{1,0:T(8,128)(2,1)}, u32[]{:S(2)}, u32[]{:S(2)}) collective-permute-start(bf16[256,1024]{1,0:T(8,128)(2,1)S(1)} %collective-permute-done.6.refs_2_), channel_id=1, source_target_pairs={{0,8},{1,9},{2,10},{3,11},{4,12},{5,13},{6,14},{7,15},{8,16},{9,17... | collective-permute-start | bytes 1572872 | tf_op jit(solution)/shard_map/ppermute | solution.py:321
  85.5 17.6 %collective-permute-start.11 = (bf16[256,1024]{1,0:T(8,128)(2,1)S(1)}, bf16[256,1024]{1,0:T(8,128)(2,1)}, u32[]{:S(2)}, u32[]{:S(2)}) collective-permute-start(bf16[256,1024]{1,0:T(8,128)(2,1)S(1)} %collective-permute-done.9.refs_5_), channel_id=1, source_target_pairs={{0,24},{1,25},{2,26},{3,27},{4,28},{5,29},{6,30},{7,31},{8,0},{9,1... | collective-permute-start | bytes 1572872 | tf_op jit(solution)/shard_map/ppermute | solution.py:322
  90.1 12.8 %collective-permute-start.15 = (bf16[16,104,128]{2,1,0:T(8,128)(2,1)S(1)}, bf16[16,104,128]{2,1,0:T(8,128)(2,1)S(1)}, u32[]{:S(2)}, u32[]{:S(2)}) collective-permute-start(bf16[16,104,128]{2,1,0:T(8,128)(2,1)S(1)} %all-to-all-done.mine_ref), channel_id=1, source_target_pairs={{0,32},{32,0},{1,33},{33,1},{2,34},{34,2},{3,35},{35,3},{4,36},{36... | collective-permute-start | bytes 1277960 | tf_op jit(solution)/shard_map/ppermute | solution.py:308
  107.7 34.0 %copy-start.1 = (bf16[64,8,128]{2,1,0:T(8,128)(2,1)S(1)}, bf16[64,8,128]{2,1,0:T(8,128)(2,1)}, u32[]{:S(2)}) copy-start(bf16[64,8,128]{2,1,0:T(8,128)(2,1)} %param.6) | copy-start | bytes 393220
  107.7 7.5 %collective-permute-start.16 = (bf16[200,1024]{1,0:T(8,128)(2,1)S(1)}, bf16[200,1024]{1,0:T(8,128)(2,1)S(1)}, u32[]{:S(2)}, u32[]{:S(2)}) collective-permute-start(bf16[200,1024]{1,0:T(8,128)(2,1)S(1)} %shard_map.70.refs_11_), channel_id=1, source_target_pairs={{0,32},{32,0},{1,33},{33,1},{2,34},{34,2},{3,35},{35,3},{4,36},{36... | collective-permute-start | bytes 1228808 | tf_op jit(solution)/shard_map/ppermute | solution.py:335
  119.9 3.3 %collective-permute-start.17 = (bf16[8,64,128]{2,1,0:T(8,128)(2,1)S(1)}, bf16[8,64,128]{2,1,0:T(8,128)(2,1)S(1)}, u32[]{:S(2)}, u32[]{:S(2)}) collective-permute-start(bf16[8,64,128]{2,1,0:T(8,128)(2,1)S(1)} %get-tuple-element.18), channel_id=1, source_target_pairs={{0,32},{32,0},{1,33},{33,1},{2,34},{34,2},{3,35},{35,3},{4,36},{36... | collective-permute-start | bytes 393224 | tf_op jit(solution)/shard_map/ppermute | solution.py:339

commit v3 on v2

--- a/solution.py
+++ b/solution.py
@@ -14,7 +14,7 @@
 F32 = jnp.float32
 VM = pltpu.VMEM
 OFFS = (0, -1, 1, 2)
-ARRIVAL = tuple((o, i) for o, half in ((0, 0), (0, 2), (1, 0), (2, 0), (1, 2), (2, 2), (3, 0), (3, 2)) for i in (half, half + 1))
+ARRIVAL = tuple((o, i) for o, half in ((0, 0), (0, 2), (1, 0), (2, 0), (2, 2), (1, 2), (3, 0), (3, 2)) for i in (half, half + 1))
 CHIPS = (0, 4, 2, 6, 1, 5, 3, 7)
 ALL = ("zl", "core", "y", "zh", "x")
 SPLIT = (8, 2, 4, 2, 4)
@@ -196,10 +196,16 @@
         acc_ref[...] += jnp.dot(jnp.concatenate(parts, axis=1), block, preferred_element_type=F32)
 
 
-def first_kernel(*refs):
-    blocks, (state_ref, coef_ref, wr_ref, out_ref, f_ref, acc_ref) = refs[:8], refs[8:]
+def early_kernel(*refs):
+    blocks, (state_ref, coef_ref, wr_ref, acc_ref, f_ref) = refs[:5], refs[5:]
     acc_ref[...] = jnp.zeros_like(acc_ref)
     sweep(state_ref[...], blocks, coef_ref, wr_ref, f_ref, acc_ref, 200, 0)
+
+
+def late_kernel(*refs):
+    blocks, (state_ref, coef_ref, wr_ref, sum_ref, out_ref, f_ref, acc_ref) = refs[:3], refs[3:]
+    acc_ref[...] = sum_ref[...]
+    sweep(state_ref[...], blocks, coef_ref, wr_ref, f_ref, acc_ref, 200, 0, 10)
     out_ref[...] = acc_ref[...].astype(BF)
 
 
@@ -251,7 +257,7 @@
 
 def call(kernel, outs, scratch, scalars, *args):
     specs = [SMEM] * scalars + [WHOLE] * (len(args) - scalars)
-    if kernel in (first_kernel, second_kernel):
+    if kernel in (early_kernel, late_kernel, second_kernel):
         args = [pltpu.with_memory_space_constraint(a, pltpu.VMEM) if a.size >= 1 << 17 else a for a in args]
     single = not isinstance(outs, (list, tuple))
     return pl.pallas_call(
@@ -320,7 +326,7 @@
     away_less = lax.ppermute(away, ALL, fwd)
     near_far = lax.ppermute(near_less, ALL, fwd)
     away_far = lax.ppermute(away_more, ALL, bwd)
-    blocks = (near, away, near_less, near_more, away_less, away_more, near_far, away_far)
+    blocks = (near, away, near_less, near_more, away_more, away_less, near_far, away_far)
 
     coef, wr = call(
         coef_kernel,
@@ -331,7 +337,8 @@
     )
     state = call(state_kernel, shape((240, 1024), BF), [VM((240, 128), F32)], 0, mine, theirs)
     scratch = [VM((2, 240, 128), F32), VM((200, 1024), F32)]
-    own = call(first_kernel, shape((200, 1024), BF), scratch, 0, *blocks, state, coef, wr)
+    part = call(early_kernel, shape((200, 1024), F32), scratch[:1], 0, *blocks[:5], state, coef, wr)
+    own = call(late_kernel, shape((200, 1024), BF), scratch, 0, *blocks[5:], state, coef, wr, part)
     other = lax.ppermute(own, "core", [(0, 1), (1, 0)])
     scratch = [VM((2, 200, 128), F32), VM((160, 1024), F32)]
     outs = [shape((8, 64, 128), F32), shape((8, 64, 128), BF)]

time: 144 us -> 142 us (0.986)
  starting transfers between devices: 81.1 us -> 78.9 us
    ppermute x1, starting transfers between devices: 6.18 us -> 4.02 us  [update(): other = lax.ppermute(own, 'core', [(0, 1), (1, 0)])]
    pallas_call x10 -> x11, Pallas kernels: 13.9 us -> 14.6 us  [call(): pl.pallas_call(kernel, out_shape=outs, in_specs=specs, out_specs=WHOLE if...]
  transfers between devices with their start and end apart: 19 -> 19, of which waited for: 6 -> 6; matrix products, arithmetic and copies ran while one was open for 1% -> 1% of each run, Pallas kernels for 3% -> 4%
where the time goes in v3:
time: 142 us; the launch traced here: 141 us
  starting transfers between devices  78.9 us (56%)
  waiting for transfers between devices  25.4 us (18%)
  blocking collectives  18.5 us (13%)
  Pallas kernels  14.6 us (10%)
  local copies, waits for them, and re-layouts  2.51 us (2%)
    all_to_all x1, blocking collectives, update(): back = lax.all_to_all(out, 'zl', 0, 0, tiled=True)  18.5 us
    ppermute x3, waiting for transfers between devices, update(): got = lax.ppermute(shard, 'zl', [(i, i ^ hop) for i in range(8)])  18 us
    ppermute x3, starting transfers between devices, update(): got = lax.ppermute(shard, 'zl', [(i, i ^ hop) for i in range(8)])  17.8 us
    pallas_call x11, Pallas kernels, call(): pl.pallas_call(kernel, out_shape=outs, in_specs=specs, out_specs=WHOLE if...  14.6 us
    ppermute x1, starting transfers between devices, update(): theirs = lax.ppermute(mine, 'core', [(0, 1), (1, 0)])  11 us
    all_to_all x1, starting transfers between devices, update(): mine = lax.all_to_all(patch, ('zh', 'zl'), 0, 0, tiled=True)  10.2 us
    ppermute x1, starting transfers between devices, update(): away_far = lax.ppermute(away_more, ALL, bwd)  4.57 us
    ppermute x1, starting transfers between devices, update(): other = lax.ppermute(own, 'core', [(0, 1), (1, 0)])  4.02 us
  transfers between devices with their start and end apart: 19, of which 6 were waited for; matrix products, arithmetic and copies ran while one was open for 1% of the time, Pallas kernels for 4%

profile of v3, /device:TPU:1, one launch (start us, length us, event | category | flops | bytes accessed | tf_op | source)
XLA Modules:
  0.0 141.1 jit_solution(14720562016855301343)
XLA Ops:
  0.8 9.6 %collective-permute-start = (bf16[16,1024]{1,0:T(8,128)(2,1)S(1)}, bf16[16,1024]{1,0:T(8,128)(2,1)S(1)}, u32[]{:S(2)}, u32[]{:S(2)}) collective-permute-start(bf16[16,1024]{1,0:T(8,128)(2,1)S(1)} %get-tuple-element.20), channel_id=1, source_target_pairs={{0,256},{64,320},{128,384},{192,448},{256,0},{320,64},{384,128},{4... | collective-permute-start | bytes 98312 | tf_op jit(solution)/shard_map/ppermute | solution.py:279
  10.4 0.9 copy-done
  12.1 1.3 collective-permute-start.12
  13.7 4.9 %collective-permute-start.1 = (bf16[32,1024]{1,0:T(8,128)(2,1)S(1)}, bf16[32,1024]{1,0:T(8,128)(2,1)S(1)}, u32[]{:S(2)}, u32[]{:S(2)}) collective-permute-start(bf16[32,1024]{1,0:T(8,128)(2,1)S(1)} %pad_maximum_fusion.2), channel_id=1, source_target_pairs={{0,128},{64,192},{128,0},{192,64},{256,384},{320,448},{384,256},{4... | collective-permute-start | bytes 196616 | tf_op jit(solution)/shard_map/ppermute | solution.py:279
  18.7 3.1 %collective-permute-start.13 = (bf16[80,128]{1,0:T(8,128)(2,1)S(1)}, bf16[80,128]{1,0:T(8,128)(2,1)S(1)}, u32[]{:S(2)}, u32[]{:S(2)}) collective-permute-start(bf16[80,128]{1,0:T(8,128)(2,1)S(1)} %get-tuple-element.13), channel_id=1, source_target_pairs={{0,1},{1,2},{2,3},{4,5},{5,6},{6,7},{8,9},{9,10},{10,11},{12,13},{... | collective-permute-start | bytes 61448 | tf_op jit(solution)/shard_map/ppermute | solution.py:300
  21.8 1.3 collective-permute-start.14
  23.9 2.5 %collective-permute-done.14.right_ref = bf16[80,128]{1,0:T(8,128)(2,1)S(1)} collective-permute-done((bf16[80,128]{1,0:T(8,128)(2,1)S(1)}, bf16[80,128]{1,0:T(8,128)(2,1)S(1)}, u32[]{:S(2)}, u32[]{:S(2)}) %collective-permute-start.14) | collective-permute-done | bytes 20512 | tf_op jit(solution)/shard_map/ppermute | solution.py:301
  26.4 1.5 %shard_map.67 = bf16[16,104,128]{2,1,0:T(8,128)(2,1)} custom-call(f32[10,144,128]{2,1,0:T(8,128)S(1)} %get-tuple-element.12.full_ref, bf16[80,128]{1,0:T(8,128)(2,1)S(1)} %collective-permute-done.13.left_ref, bf16[80,128]{1,0:T(8,128)(2,1)S(1)} %collective-permute-done.14.right_ref, f32[20,128]{1,0:T(8,128)S(1)} %reshape.14.pars_ref), custom_call_target="tpu_custom_call" | custom-call | tf_op jit(solution)/shard_map/pallas_call | solution.py:263
  27.8 10.2 %all-to-all-start = ((bf16[16,104,128]{2,1,0:T(8,128)(2,1)}), bf16[16,104,128]{2,1,0:T(8,128)(2,1)S(1)}, u32[]{:S(2)}, u32[]{:S(2)}) async-start(bf16[16,104,128]{2,1,0:T(8,128)(2,1)} %shard_map.67), calls=%async_computation | async-start | bytes 851968 | tf_op jit(solution)/shard_map/all_to_all | solution.py:313
  38.1 3.3 %collective-permute-start.2 = (bf16[64,1024]{1,0:T(8,128)(2,1)S(1)}, bf16[64,1024]{1,0:T(8,128)(2,1)S(1)}, u32[]{:S(2)}, u32[]{:S(2)}) collective-permute-start(bf16[64,1024]{1,0:T(8,128)(2,1)S(1)} %pad_maximum_fusion.1), channel_id=1, source_target_pairs={{0,64},{64,0},{128,192},{192,128},{256,320},{320,256},{384,448},{4... | collective-permute-start | bytes 393224 | tf_op jit(solution)/shard_map/ppermute | solution.py:279
  41.4 18.0 %collective-permute-done.2 = bf16[64,1024]{1,0:T(8,128)(2,1)S(1)} collective-permute-done((bf16[64,1024]{1,0:T(8,128)(2,1)S(1)}, bf16[64,1024]{1,0:T(8,128)(2,1)S(1)}, u32[]{:S(2)}, u32[]{:S(2)}) %collective-permute-start.2) | collective-permute-done | bytes 131104 | tf_op jit(solution)/shard_map/ppermute | solution.py:279
  59.4 3.2 %collective-permute-start.3 = (bf16[128,1024]{1,0:T(8,128)(2,1)S(1)}, bf16[128,1024]{1,0:T(8,128)(2,1)S(1)}, u32[]{:S(2)}, u32[]{:S(2)}) collective-permute-start(bf16[128,1024]{1,0:T(8,128)(2,1)S(1)} %pad_maximum_fusion), channel_id=1, source_target_pairs={{0,1},{1,2},{2,3},{3,0},{4,5},{5,6},{6,7},{7,4},{8,9},{9,10},{10,1... | collective-permute-start | bytes 786440 | tf_op jit(solution)/shard_map/ppermute | solution.py:317
  62.6 3.3 %collective-permute-start.4 = (bf16[128,1024]{1,0:T(8,128)(2,1)S(1)}, bf16[128,1024]{1,0:T(8,128)(2,1)S(1)}, u32[]{:S(2)}, u32[]{:S(2)}) collective-permute-start(bf16[128,1024]{1,0:T(8,128)(2,1)S(1)} %pad_maximum_fusion), channel_id=1, source_target_pairs={{0,3},{1,0},{2,1},{3,2},{4,7},{5,4},{6,5},{7,6},{8,11},{9,8},{10,9... | collective-permute-start | bytes 786440 | tf_op jit(solution)/shard_map/ppermute | solution.py:318
  65.9 3.3 %collective-permute-start.5 = (bf16[128,1024]{1,0:T(8,128)(2,1)S(1)}, bf16[128,1024]{1,0:T(8,128)(2,1)S(1)}, u32[]{:S(2)}, u32[]{:S(2)}) collective-permute-start(bf16[128,1024]{1,0:T(8,128)(2,1)S(1)} %pad_maximum_fusion), channel_id=1, source_target_pairs={{0,2},{1,3},{2,0},{3,1},{4,6},{5,7},{6,4},{7,5},{8,10},{9,11},{10,... | collective-permute-start | bytes 786440 | tf_op jit(solution)/shard_map/ppermute | solution.py:320
  69.3 3.1 %collective-permute-start.6 = (bf16[256,1024]{1,0:T(8,128)(2,1)S(1)}, bf16[256,1024]{1,0:T(8,128)(2,1)S(1)}, u32[]{:S(2)}, u32[]{:S(2)}) collective-permute-start(bf16[256,1024]{1,0:T(8,128)(2,1)S(1)} %constant_dynamic-update-slice_fusion.refs_0_), channel_id=1, source_target_pairs={{0,8},{1,9},{2,10},{3,11},{4,12},{5,13},{6,14},{7,15},{8,16},{9,17... | collective-permute-start | bytes 1572872 | tf_op jit(solution)/shard_map/ppermute | solution.py:322
  72.5 2.0 %collective-permute-done.5 = bf16[128,1024]{1,0:T(8,128)(2,1)S(1)} collective-permute-done((bf16[128,1024]{1,0:T(8,128)(2,1)S(1)}, bf16[128,1024]{1,0:T(8,128)(2,1)S(1)}, u32[]{:S(2)}, u32[]{:S(2)}) %collective-permute-start.5) | collective-permute-done | bytes 262176 | tf_op jit(solution)/shard_map/ppermute | solution.py:320
  74.6 2.9 %collective-permute-start.8 = (bf16[256,1024]{1,0:T(8,128)(2,1)S(1)}, bf16[256,1024]{1,0:T(8,128)(2,1)S(1)}, u32[]{:S(2)}, u32[]{:S(2)}) collective-permute-start(bf16[256,1024]{1,0:T(8,128)(2,1)S(1)} %constant_dynamic-update-slice_fusion.5.refs_1_), channel_id=1, source_target_pairs={{0,24},{1,25},{2,26},{3,27},{4,28},{5,29},{6,30},{7,31},{8,0},{9,1... | collective-permute-start | bytes 1572872 | tf_op jit(solution)/shard_map/ppermute | solution.py:325
  77.5 3.6 %collective-permute-start.7 = (bf16[256,1024]{1,0:T(8,128)(2,1)S(1)}, bf16[256,1024]{1,0:T(8,128)(2,1)S(1)}, u32[]{:S(2)}, u32[]{:S(2)}) collective-permute-start(bf16[256,1024]{1,0:T(8,128)(2,1)S(1)} %constant_dynamic-update-slice_fusion.refs_0_), channel_id=1, source_target_pairs={{0,24},{1,25},{2,26},{3,27},{4,28},{5,29},{6,30},{7,31},{8,0},{9,1... | collective-permute-start | bytes 1572872 | tf_op jit(solution)/shard_map/ppermute | solution.py:323
  81.1 1.9 %collective-permute-start.9 = (bf16[256,1024]{1,0:T(8,128)(2,1)S(1)}, bf16[256,1024]{1,0:T(8,128)(2,1)}, u32[]{:S(2)}, u32[]{:S(2)}) collective-permute-start(bf16[256,1024]{1,0:T(8,128)(2,1)S(1)} %constant_dynamic-update-slice_fusion.5.refs_1_), channel_id=1, source_target_pairs={{0,8},{1,9},{2,10},{3,11},{4,12},{5,13},{6,14},{7,15},{8,16},{9,17... | collective-permute-start | bytes 1572872 | tf_op jit(solution)/shard_map/ppermute | solution.py:326
  83.6 1.9 %collective-permute-start.10 = (bf16[256,1024]{1,0:T(8,128)(2,1)S(1)}, bf16[256,1024]{1,0:T(8,128)(2,1)}, u32[]{:S(2)}, u32[]{:S(2)}) collective-permute-start(bf16[256,1024]{1,0:T(8,128)(2,1)S(1)} %collective-permute-done.6.refs_2_), channel_id=1, source_target_pairs={{0,8},{1,9},{2,10},{3,11},{4,12},{5,13},{6,14},{7,15},{8,16},{9,17... | collective-permute-start | bytes 1572872 | tf_op jit(solution)/shard_map/ppermute | solution.py:327
  85.5 4.6 %collective-permute-start.11 = (bf16[256,1024]{1,0:T(8,128)(2,1)S(1)}, bf16[256,1024]{1,0:T(8,128)(2,1)}, u32[]{:S(2)}, u32[]{:S(2)}) collective-permute-start(bf16[256,1024]{1,0:T(8,128)(2,1)S(1)} %collective-permute-done.8.refs_4_), channel_id=1, source_target_pairs={{0,24},{1,25},{2,26},{3,27},{4,28},{5,29},{6,30},{7,31},{8,0},{9,1... | collective-permute-start | bytes 1572872 | tf_op jit(solution)/shard_map/ppermute | solution.py:328
  90.1 11.0 %collective-permute-start.15 = (bf16[16,104,128]{2,1,0:T(8,128)(2,1)S(1)}, bf16[16,104,128]{2,1,0:T(8,128)(2,1)S(1)}, u32[]{:S(2)}, u32[]{:S(2)}) collective-permute-start(bf16[16,104,128]{2,1,0:T(8,128)(2,1)S(1)} %all-to-all-done.mine_ref), channel_id=1, source_target_pairs={{0,32},{32,0},{1,33},{33,1},{2,34},{34,2},{3,35},{35,3},{4,36},{36... | collective-permute-start | bytes 1277960 | tf_op jit(solution)/shard_map/ppermute | solution.py:314
  101.1 1.8 %shard_map.69 = (f32[16,240,128]{2,1,0:T(8,128)S(1)}, f32[2,16,128]{2,1,0:T(8,128)S(1)}) custom-call(bf16[16,104,128]{2,1,0:T(8,128)(2,1)S(1)} %all-to-all-done.mine_ref), custom_call_target="tpu_custom_call" | custom-call | tf_op jit(solution)/shard_map/pallas_call | solution.py:263
  103.1 2.2 %shard_map.70.refs_6_ = f32[200,1024]{1,0:T(8,128)S(1)} custom-call(bf16[256,1024]{1,0:T(8,128)(2,1)S(1)} %constant_dynamic-update-slice_fusion.refs_0_, bf16[256,1024]{1,0:T(8,128)(2,1)S(1)} %constant_dynamic-update-slice_fusion.5.refs_1_, bf16[256,1024]{1,0:T(8,128)(2,1)S(1)} %collective-permute-done.6.refs_2_, ...), custom_call_target="tpu_custom_call" | custom-call | tf_op jit(solution)/shard_map/pallas_call | solution.py:263
  105.3 3.0 %shard_map.71.refs_11_ = bf16[200,1024]{1,0:T(8,128)(2,1)S(1)} custom-call(bf16[256,1024]{1,0:T(8,128)(2,1)} %collective-permute-done.9.refs_0_.refs_5_, bf16[256,1024]{1,0:T(8,128)(2,1)} %collective-permute-done.10.refs_1_.refs_6_, bf16[256,1024]{1,0:T(8,128)(2,1)} %collective-permute-done.11.refs_2_.refs_7_, ...), custom_call_target="tpu_custom_call" | custom-call | tf_op jit(solution)/shard_map/pallas_call | solution.py:263
  108.4 4.0 %collective-permute-start.16 = (bf16[200,1024]{1,0:T(8,128)(2,1)S(1)}, bf16[200,1024]{1,0:T(8,128)(2,1)S(1)}, u32[]{:S(2)}, u32[]{:S(2)}) collective-permute-start(bf16[200,1024]{1,0:T(8,128)(2,1)S(1)} %shard_map.71.refs_11_), channel_id=1, source_target_pairs={{0,32},{32,0},{1,33},{33,1},{2,34},{34,2},{3,35},{35,3},{4,36},{36... | collective-permute-start | bytes 1228808 | tf_op jit(solution)/shard_map/ppermute | solution.py:342
  112.4 1.4 collective-permute-done.16.refs_12_
  113.8 4.6 %shard_map.72 = (f32[8,64,128]{2,1,0:T(8,128)S(1)}, bf16[8,64,128]{2,1,0:T(8,128)(2,1)S(1)}) custom-call(bf16[256,1024]{1,0:T(8,128)(2,1)S(1)} %constant_dynamic-update-slice_fusion.refs_0_, bf16[256,1024]{1,0:T(8,128)(2,1)S(1)} %constant_dynamic-update-slice_fusion.5.refs_1_, bf16[256,1024]{1,0:T(8,128)(2,1)S(1)} %collective-permute-done.6.refs_2_, ...), custom_call_target="tpu_custom_call" | custom-call | tf_op jit(solution)/shard_map/pallas_call | solution.py:263
  118.4 2.3 %collective-permute-start.17 = (bf16[8,64,128]{2,1,0:T(8,128)(2,1)S(1)}, bf16[8,64,128]{2,1,0:T(8,128)(2,1)S(1)}, u32[]{:S(2)}, u32[]{:S(2)}) collective-permute-start(bf16[8,64,128]{2,1,0:T(8,128)(2,1)S(1)} %get-tuple-element.18), channel_id=1, source_target_pairs={{0,32},{32,0},{1,33},{33,1},{2,34},{34,2},{3,35},{35,3},{4,36},{36... | collective-permute-start | bytes 393224 | tf_op jit(solution)/shard_map/ppermute | solution.py:346
  120.7 1.0 collective-permute-done.17.got_ref
  121.7 18.5 %all_to_all.10.back_ref = bf16[8,64,128]{2,1,0:T(8,128)(2,1)S(1)} all-to-all(bf16[8,64,128]{2,1,0:T(8,128)(2,1)S(1)} %shard_map.73), channel_id=1, replica_groups=mesh['zl'=8,'core'=2,'y'=4,'zh'=2,'x'=4] {'zl'}, dimensions={0} | all-to-all | bytes 262144 | tf_op jit(solution)/shard_map/all_to_all | solution.py:348
  140.2 0.8 shard_map.74
  (36 shorter events, 3.6 us)
Async XLA Ops:
  0.8 12.9 %collective-permute-start = (bf16[16,1024]{1,0:T(8,128)(2,1)S(1)}, bf16[16,1024]{1,0:T(8,128)(2,1)S(1)}, u32[]{:S(2)}, u32[]{:S(2)}) collective-permute-start(bf16[16,1024]{1,0:T(8,128)(2,1)S(1)} %get-tuple-element.20), channel_id=1, source_target_pairs={{0,256},{64,320},{128,384},{192,448},{256,0},{320,64},{384,128},{4... | collective-permute-start | bytes 98312 | tf_op jit(solution)/shard_map/ppermute | solution.py:279
  10.4 0.9 copy-start
  11.3 0.8 copy-start.2
  12.1 6.5 %collective-permute-start.12 = (bf16[160,128]{1,0:T(8,128)(2,1)S(1)}, bf16[160,128]{1,0:T(8,128)(2,1)S(1)}, u32[]{:S(2)}, u32[]{:S(2)}) collective-permute-start(bf16[160,128]{1,0:T(8,128)(2,1)S(1)} %shard_map.65), channel_id=1, source_target_pairs={{4,12},{5,13},{6,14},{7,15},{8,0},{9,1},{10,2},{11,3},{12,20},{13,... | collective-permute-start | bytes 122888 | tf_op jit(solution)/shard_map/ppermute | solution.py:289
  13.7 24.4 %collective-permute-start.1 = (bf16[32,1024]{1,0:T(8,128)(2,1)S(1)}, bf16[32,1024]{1,0:T(8,128)(2,1)S(1)}, u32[]{:S(2)}, u32[]{:S(2)}) collective-permute-start(bf16[32,1024]{1,0:T(8,128)(2,1)S(1)} %pad_maximum_fusion.2), channel_id=1, source_target_pairs={{0,128},{64,192},{128,0},{192,64},{256,384},{320,448},{384,256},{4... | collective-permute-start | bytes 196616 | tf_op jit(solution)/shard_map/ppermute | solution.py:279
  18.7 5.2 %collective-permute-start.13 = (bf16[80,128]{1,0:T(8,128)(2,1)S(1)}, bf16[80,128]{1,0:T(8,128)(2,1)S(1)}, u32[]{:S(2)}, u32[]{:S(2)}) collective-permute-start(bf16[80,128]{1,0:T(8,128)(2,1)S(1)} %get-tuple-element.13), channel_id=1, source_target_pairs={{0,1},{1,2},{2,3},{4,5},{5,6},{6,7},{8,9},{9,10},{10,11},{12,13},{... | collective-permute-start | bytes 61448 | tf_op jit(solution)/shard_map/ppermute | solution.py:300
  21.8 4.5 %collective-permute-start.14 = (bf16[80,128]{1,0:T(8,128)(2,1)S(1)}, bf16[80,128]{1,0:T(8,128)(2,1)S(1)}, u32[]{:S(2)}, u32[]{:S(2)}) collective-permute-start(bf16[80,128]{1,0:T(8,128)(2,1)S(1)} %get-tuple-element.14), channel_id=1, source_target_pairs={{1,0},{2,1},{3,2},{5,4},{6,5},{7,6},{9,8},{10,9},{11,10},{13,12},{... | collective-permute-start | bytes 61448 | tf_op jit(solution)/shard_map/ppermute | solution.py:301
  27.8 62.3 %all-to-all-start = ((bf16[16,104,128]{2,1,0:T(8,128)(2,1)}), bf16[16,104,128]{2,1,0:T(8,128)(2,1)S(1)}, u32[]{:S(2)}, u32[]{:S(2)}) async-start(bf16[16,104,128]{2,1,0:T(8,128)(2,1)} %shard_map.67), calls=%async_computation | async-start | bytes 851968 | tf_op jit(solution)/shard_map/all_to_all | solution.py:313
  38.1 21.3 %collective-permute-start.2 = (bf16[64,1024]{1,0:T(8,128)(2,1)S(1)}, bf16[64,1024]{1,0:T(8,128)(2,1)S(1)}, u32[]{:S(2)}, u32[]{:S(2)}) collective-permute-start(bf16[64,1024]{1,0:T(8,128)(2,1)S(1)} %pad_maximum_fusion.1), channel_id=1, source_target_pairs={{0,64},{64,0},{128,192},{192,128},{256,320},{320,256},{384,448},{4... | collective-permute-start | bytes 393224 | tf_op jit(solution)/shard_map/ppermute | solution.py:279
  59.4 9.9 %collective-permute-start.3 = (bf16[128,1024]{1,0:T(8,128)(2,1)S(1)}, bf16[128,1024]{1,0:T(8,128)(2,1)S(1)}, u32[]{:S(2)}, u32[]{:S(2)}) collective-permute-start(bf16[128,1024]{1,0:T(8,128)(2,1)S(1)} %pad_maximum_fusion), channel_id=1, source_target_pairs={{0,1},{1,2},{2,3},{3,0},{4,5},{5,6},{6,7},{7,4},{8,9},{9,10},{10,1... | collective-permute-start | bytes 786440 | tf_op jit(solution)/shard_map/ppermute | solution.py:317
  62.6 9.9 %collective-permute-start.4 = (bf16[128,1024]{1,0:T(8,128)(2,1)S(1)}, bf16[128,1024]{1,0:T(8,128)(2,1)S(1)}, u32[]{:S(2)}, u32[]{:S(2)}) collective-permute-start(bf16[128,1024]{1,0:T(8,128)(2,1)S(1)} %pad_maximum_fusion), channel_id=1, source_target_pairs={{0,3},{1,0},{2,1},{3,2},{4,7},{5,4},{6,5},{7,6},{8,11},{9,8},{10,9... | collective-permute-start | bytes 786440 | tf_op jit(solution)/shard_map/ppermute | solution.py:318
  65.9 8.6 %collective-permute-start.5 = (bf16[128,1024]{1,0:T(8,128)(2,1)S(1)}, bf16[128,1024]{1,0:T(8,128)(2,1)S(1)}, u32[]{:S(2)}, u32[]{:S(2)}) collective-permute-start(bf16[128,1024]{1,0:T(8,128)(2,1)S(1)} %pad_maximum_fusion), channel_id=1, source_target_pairs={{0,2},{1,3},{2,0},{3,1},{4,6},{5,7},{6,4},{7,5},{8,10},{9,11},{10,... | collective-permute-start | bytes 786440 | tf_op jit(solution)/shard_map/ppermute | solution.py:320
  69.3 14.2 %collective-permute-start.6 = (bf16[256,1024]{1,0:T(8,128)(2,1)S(1)}, bf16[256,1024]{1,0:T(8,128)(2,1)S(1)}, u32[]{:S(2)}, u32[]{:S(2)}) collective-permute-start(bf16[256,1024]{1,0:T(8,128)(2,1)S(1)} %constant_dynamic-update-slice_fusion.refs_0_), channel_id=1, source_target_pairs={{0,8},{1,9},{2,10},{3,11},{4,12},{5,13},{6,14},{7,15},{8,16},{9,17... | collective-permute-start | bytes 1572872 | tf_op jit(solution)/shard_map/ppermute | solution.py:322
  74.6 10.9 %collective-permute-start.8 = (bf16[256,1024]{1,0:T(8,128)(2,1)S(1)}, bf16[256,1024]{1,0:T(8,128)(2,1)S(1)}, u32[]{:S(2)}, u32[]{:S(2)}) collective-permute-start(bf16[256,1024]{1,0:T(8,128)(2,1)S(1)} %constant_dynamic-update-slice_fusion.5.refs_1_), channel_id=1, source_target_pairs={{0,24},{1,25},{2,26},{3,27},{4,28},{5,29},{6,30},{7,31},{8,0},{9,1... | collective-permute-start | bytes 1572872 | tf_op jit(solution)/shard_map/ppermute | solution.py:325
  77.5 25.6 %collective-permute-start.7 = (bf16[256,1024]{1,0:T(8,128)(2,1)S(1)}, bf16[256,1024]{1,0:T(8,128)(2,1)S(1)}, u32[]{:S(2)}, u32[]{:S(2)}) collective-permute-start(bf16[256,1024]{1,0:T(8,128)(2,1)S(1)} %constant_dynamic-update-slice_fusion.refs_0_), channel_id=1, source_target_pairs={{0,24},{1,25},{2,26},{3,27},{4,28},{5,29},{6,30},{7,31},{8,0},{9,1... | collective-permute-start | bytes 1572872 | tf_op jit(solution)/shard_map/ppermute | solution.py:323
  81.1 24.1 %collective-permute-start.9 = (bf16[256,1024]{1,0:T(8,128)(2,1)S(1)}, bf16[256,1024]{1,0:T(8,128)(2,1)}, u32[]{:S(2)}, u32[]{:S(2)}) collective-permute-start(bf16[256,1024]{1,0:T(8,128)(2,1)S(1)} %constant_dynamic-update-slice_fusion.5.refs_1_), channel_id=1, source_target_pairs={{0,8},{1,9},{2,10},{3,11},{4,12},{5,13},{6,14},{7,15},{8,16},{9,17... | collective-permute-start | bytes 1572872 | tf_op jit(solution)/shard_map/ppermute | solution.py:326
  83.6 21.7 %collective-permute-start.10 = (bf16[256,1024]{1,0:T(8,128)(2,1)S(1)}, bf16[256,1024]{1,0:T(8,128)(2,1)}, u32[]{:S(2)}, u32[]{:S(2)}) collective-permute-start(bf16[256,1024]{1,0:T(8,128)(2,1)S(1)} %collective-permute-done.6.refs_2_), channel_id=1, source_target_pairs={{0,8},{1,9},{2,10},{3,11},{4,12},{5,13},{6,14},{7,15},{8,16},{9,17... | collective-permute-start | bytes 1572872 | tf_op jit(solution)/shard_map/ppermute | solution.py:327
  85.5 19.8 %collective-permute-start.11 = (bf16[256,1024]{1,0:T(8,128)(2,1)S(1)}, bf16[256,1024]{1,0:T(8,128)(2,1)}, u32[]{:S(2)}, u32[]{:S(2)}) collective-permute-start(bf16[256,1024]{1,0:T(8,128)(2,1)S(1)} %collective-permute-done.8.refs_4_), channel_id=1, source_target_pairs={{0,24},{1,25},{2,26},{3,27},{4,28},{5,29},{6,30},{7,31},{8,0},{9,1... | collective-permute-start | bytes 1572872 | tf_op jit(solution)/shard_map/ppermute | solution.py:328
  90.1 12.8 %collective-permute-start.15 = (bf16[16,104,128]{2,1,0:T(8,128)(2,1)S(1)}, bf16[16,104,128]{2,1,0:T(8,128)(2,1)S(1)}, u32[]{:S(2)}, u32[]{:S(2)}) collective-permute-start(bf16[16,104,128]{2,1,0:T(8,128)(2,1)S(1)} %all-to-all-done.mine_ref), channel_id=1, source_target_pairs={{0,32},{32,0},{1,33},{33,1},{2,34},{34,2},{3,35},{35,3},{4,36},{36... | collective-permute-start | bytes 1277960 | tf_op jit(solution)/shard_map/ppermute | solution.py:314
  108.4 31.9 %copy-start.1 = (bf16[64,8,128]{2,1,0:T(8,128)(2,1)S(1)}, bf16[64,8,128]{2,1,0:T(8,128)(2,1)}, u32[]{:S(2)}) copy-start(bf16[64,8,128]{2,1,0:T(8,128)(2,1)} %param.6) | copy-start | bytes 393220
  108.4 5.4 %collective-permute-start.16 = (bf16[200,1024]{1,0:T(8,128)(2,1)S(1)}, bf16[200,1024]{1,0:T(8,128)(2,1)S(1)}, u32[]{:S(2)}, u32[]{:S(2)}) collective-permute-start(bf16[200,1024]{1,0:T(8,128)(2,1)S(1)} %shard_map.71.refs_11_), channel_id=1, source_target_pairs={{0,32},{32,0},{1,33},{33,1},{2,34},{34,2},{3,35},{35,3},{4,36},{36... | collective-permute-start | bytes 1228808 | tf_op jit(solution)/shard_map/ppermute | solution.py:342
  118.4 3.3 %collective-permute-start.17 = (bf16[8,64,128]{2,1,0:T(8,128)(2,1)S(1)}, bf16[8,64,128]{2,1,0:T(8,128)(2,1)S(1)}, u32[]{:S(2)}, u32[]{:S(2)}) collective-permute-start(bf16[8,64,128]{2,1,0:T(8,128)(2,1)S(1)} %get-tuple-element.18), channel_id=1, source_target_pairs={{0,32},{32,0},{1,33},{33,1},{2,34},{34,2},{3,35},{35,3},{4,36},{36... | collective-permute-start | bytes 393224 | tf_op jit(solution)/shard_map/ppermute | solution.py:346

commit v4 on v3

--- a/solution.py
+++ b/solution.py
@@ -93,7 +93,9 @@
     return logs
 
 
-def patches_kernel(full_ref, left_ref, right_ref, pars_ref, send_ref, wide_ref, cell_ref, scr_ref):
+def patches_kernel(
+    full_ref, left_ref, right_ref, weights_ref, rates_ref, nodes_ref, send_ref, wide_ref, cell_ref, scr_ref, pars_ref
+):
     left, right = left_ref[...].astype(F32), right_ref[...].astype(F32)
     for r in range(10):
         wide_ref[r, 0:8, :] = left[r * 8 : r * 8 + 8]
@@ -107,6 +109,11 @@
         scr_ref[0:80, :] = halves(cell_ref[0:80, :], swapped(cell_ref[80:160, :]))
         scr_ref[80:100, :] = log_rows(cell_ref, 20)
         send_ref[zh * 8 + d] = scr_ref[...].astype(BF)
+    for h in range(2):
+        half = slice(h * 128, h * 128 + 128)
+        pars_ref[h : h + 1, :] = weights_ref[:, half]
+        pars_ref[2 + h : 3 + h, :] = rates_ref[:, half]
+        pars_ref[pl.ds(4 + h, 8, stride=2), :] = nodes_ref[:, half]
     pars = pars_ref[...]
     high = pars.astype(BF).astype(F32)
     scr_ref[56:76, :] = high
@@ -299,16 +306,17 @@
     right = [(i, i + 1) for i in range(3)]
     from_left = lax.ppermute(last, "x", right)
     from_right = lax.ppermute(lead, "x", [(j, i) for i, j in right])
-    pars = jnp.concatenate([quad_weights[None], reaction_rates[None], germ_nodes.T], axis=0).reshape(20, 128)
     patch = call(
         patches_kernel,
         shape((16, 104, 128), BF),
-        [VM((10, 144, 128), F32), VM((160, 128), F32), VM((104, 128), F32)],
+        [VM((10, 144, 128), F32), VM((160, 128), F32), VM((104, 128), F32), VM((20, 128), F32)],
         0,
         full,
         from_left,
         from_right,
-        pars,
+        quad_weights[None],
+        reaction_rates[None],
+        germ_nodes.T,
     )
     mine = lax.all_to_all(patch, ("zh", "zl"), 0, 0, tiled=True)
     theirs = lax.ppermute(mine, "core", [(0, 1), (1, 0)])
@@ -317,7 +325,7 @@
     less = lax.ppermute(shard, ALL, fwd)
     more = lax.ppermute(shard, ALL, bwd)
     near = jnp.concatenate([shard, less], axis=0)
-    far = lax.ppermute(shard, ALL, plane_shift(0, 2))
+    far = lax.ppermute(less, ALL, fwd)
     fwd, bwd = plane_shift(1, 1), plane_shift(1, -1)
     near_less = lax.ppermute(near, ALL, fwd)
     near_more = lax.ppermute(near, ALL, bwd)

time: 142 us -> 131 us (0.923)
  waiting for transfers between devices: 25.4 us -> 12.1 us
    ppermute x3, waiting for transfers between devices: 18 us -> 1.29 us  [update(): got = lax.ppermute(shard, 'zl', [(i, i ^ hop) for i in range(8)])]
    ppermute x1, waiting for transfers between devices: 0.01 us -> 3.23 us  [update(): got = lax.ppermute(rows, ALL, shift(toward))]
    ppermute x1, waiting for transfers between devices: 2.48 us -> 0.01 us  [update(): from_right = lax.ppermute(lead, 'x', [(j, i) for i, j in right])]
    ppermute x1, waiting for transfers between devices: 0.01 us -> 1.79 us  [update(): less = lax.ppermute(shard, ALL, fwd)]
    ppermute x1, starting transfers between devices: 2.91 us -> 4.46 us  [update(): away_more = lax.ppermute(away, ALL, bwd)]
    ppermute x1, starting transfers between devices: 3.35 us -> 1.91 us  [update(): far = lax.ppermute(less, ALL, fwd)]
  transfers between devices with their start and end apart: 19 -> 19, of which waited for: 6 -> 6; matrix products, arithmetic and copies ran while one was open for 1% -> 0% of each run, Pallas kernels for 4% -> 5%
where the time goes in v4:
time: 131 us; the launch traced here: 130 us
  starting transfers between devices  80.2 us (61%)
  blocking collectives  19.7 us (15%)
  Pallas kernels  14.6 us (11%)
  waiting for transfers between devices  12.1 us (9%)
  local copies, waits for them, and re-layouts  2.55 us (2%)
    all_to_all x1, blocking collectives, update(): back = lax.all_to_all(out, 'zl', 0, 0, tiled=True)  19.7 us
    ppermute x3, starting transfers between devices, update(): got = lax.ppermute(shard, 'zl', [(i, i ^ hop) for i in range(8)])  18.6 us
    pallas_call x11, Pallas kernels, call(): pl.pallas_call(kernel, out_shape=outs, in_specs=specs, out_specs=WHOLE if...  14.6 us
    ppermute x1, starting transfers between devices, update(): theirs = lax.ppermute(mine, 'core', [(0, 1), (1, 0)])  11.4 us
    all_to_all x1, starting transfers between devices, update(): mine = lax.all_to_all(patch, ('zh', 'zl'), 0, 0, tiled=True)  10.2 us
    ppermute x1, starting transfers between devices, update(): away_far = lax.ppermute(away_more, ALL, bwd)  4.57 us
    ppermute x1, starting transfers between devices, update(): away_more = lax.ppermute(away, ALL, bwd)  4.46 us
    ppermute x1, starting transfers between devices, update(): less = lax.ppermute(shard, ALL, fwd)  3.95 us
  transfers between devices with their start and end apart: 19, of which 6 were waited for; matrix products, arithmetic and copies ran while one was open for 0% of the time, Pallas kernels for 5%

profile of v4, /device:TPU:1, one launch (start us, length us, event | category | flops | bytes accessed | tf_op | source)
XLA Modules:
  0.0 129.6 jit_solution(16390901254827452388)
XLA Ops:
  0.8 9.6 %collective-permute-start = (bf16[16,1024]{1,0:T(8,128)(2,1)S(1)}, bf16[16,1024]{1,0:T(8,128)(2,1)S(1)}, u32[]{:S(2)}, u32[]{:S(2)}) collective-permute-start(bf16[16,1024]{1,0:T(8,128)(2,1)S(1)} %get-tuple-element.20), channel_id=1, source_target_pairs={{0,256},{64,320},{128,384},{192,448},{256,0},{320,64},{384,128},{4... | collective-permute-start | bytes 98312 | tf_op jit(solution)/shard_map/ppermute | solution.py:286
  10.4 1.3 collective-permute-done
  11.7 4.9 %collective-permute-start.1 = (bf16[32,1024]{1,0:T(8,128)(2,1)S(1)}, bf16[32,1024]{1,0:T(8,128)(2,1)S(1)}, u32[]{:S(2)}, u32[]{:S(2)}) collective-permute-start(bf16[32,1024]{1,0:T(8,128)(2,1)S(1)} %pad_maximum_fusion.2), channel_id=1, source_target_pairs={{0,128},{64,192},{128,0},{192,64},{256,384},{320,448},{384,256},{4... | collective-permute-start | bytes 196616 | tf_op jit(solution)/shard_map/ppermute | solution.py:286
  16.6 0.9 copy-done
  18.3 1.3 collective-permute-start.12
  19.9 3.2 %collective-permute-done.12.got_ref = bf16[160,128]{1,0:T(8,128)(2,1)S(1)} collective-permute-done((bf16[160,128]{1,0:T(8,128)(2,1)S(1)}, bf16[160,128]{1,0:T(8,128)(2,1)S(1)}, u32[]{:S(2)}, u32[]{:S(2)}) %collective-permute-start.12) | collective-permute-done | bytes 40992 | tf_op jit(solution)/shard_map/ppermute | solution.py:296
  23.2 3.1 %collective-permute-start.13 = (bf16[80,128]{1,0:T(8,128)(2,1)S(1)}, bf16[80,128]{1,0:T(8,128)(2,1)S(1)}, u32[]{:S(2)}, u32[]{:S(2)}) collective-permute-start(bf16[80,128]{1,0:T(8,128)(2,1)S(1)} %get-tuple-element.13), channel_id=1, source_target_pairs={{0,1},{1,2},{2,3},{4,5},{5,6},{6,7},{8,9},{9,10},{10,11},{12,13},{... | collective-permute-start | bytes 61448 | tf_op jit(solution)/shard_map/ppermute | solution.py:307
  26.4 1.3 collective-permute-start.14
  27.7 4.0 %collective-permute-start.2 = (bf16[64,1024]{1,0:T(8,128)(2,1)S(1)}, bf16[64,1024]{1,0:T(8,128)(2,1)S(1)}, u32[]{:S(2)}, u32[]{:S(2)}) collective-permute-start(bf16[64,1024]{1,0:T(8,128)(2,1)S(1)} %pad_maximum_fusion.1), channel_id=1, source_target_pairs={{0,64},{64,0},{128,192},{192,128},{256,320},{320,256},{384,448},{4... | collective-permute-start | bytes 393224 | tf_op jit(solution)/shard_map/ppermute | solution.py:286
  31.8 1.5 %shard_map.67 = bf16[16,104,128]{2,1,0:T(8,128)(2,1)} custom-call(f32[10,144,128]{2,1,0:T(8,128)S(1)} %get-tuple-element.12.full_ref, bf16[80,128]{1,0:T(8,128)(2,1)S(1)} %collective-permute-done.13.left_ref, bf16[80,128]{1,0:T(8,128)(2,1)S(1)} %collective-permute-done.14.right_ref, f32[1,256]{1,0:T(1,128)S(1)} %bitcast.12, f32[1,256]{1,0:T(1,128)S(1)} %bitcast.13, ...), custom_call_target="tpu_custom_call" | custom-call | tf_op jit(solution)/shard_map/pallas_call | solution.py:270
  33.3 10.2 %all-to-all-start = ((bf16[16,104,128]{2,1,0:T(8,128)(2,1)}), bf16[16,104,128]{2,1,0:T(8,128)(2,1)S(1)}, u32[]{:S(2)}, u32[]{:S(2)}) async-start(bf16[16,104,128]{2,1,0:T(8,128)(2,1)} %shard_map.67), calls=%async_computation | async-start | bytes 851968 | tf_op jit(solution)/shard_map/all_to_all | solution.py:321
  43.5 4.0 %collective-permute-start.3 = (bf16[128,1024]{1,0:T(8,128)(2,1)S(1)}, bf16[128,1024]{1,0:T(8,128)(2,1)S(1)}, u32[]{:S(2)}, u32[]{:S(2)}) collective-permute-start(bf16[128,1024]{1,0:T(8,128)(2,1)S(1)} %pad_maximum_fusion), channel_id=1, source_target_pairs={{0,1},{1,2},{2,3},{3,0},{4,5},{5,6},{6,7},{7,4},{8,9},{9,10},{10,1... | collective-permute-start | bytes 786440 | tf_op jit(solution)/shard_map/ppermute | solution.py:325
  47.5 3.4 %collective-permute-start.4 = (bf16[128,1024]{1,0:T(8,128)(2,1)S(1)}, bf16[128,1024]{1,0:T(8,128)(2,1)S(1)}, u32[]{:S(2)}, u32[]{:S(2)}) collective-permute-start(bf16[128,1024]{1,0:T(8,128)(2,1)S(1)} %pad_maximum_fusion), channel_id=1, source_target_pairs={{0,3},{1,0},{2,1},{3,2},{4,7},{5,4},{6,5},{7,6},{8,11},{9,8},{10,9... | collective-permute-start | bytes 786440 | tf_op jit(solution)/shard_map/ppermute | solution.py:326
  50.9 1.8 %collective-permute-done.3 = bf16[128,1024]{1,0:T(8,128)(2,1)S(1)} collective-permute-done((bf16[128,1024]{1,0:T(8,128)(2,1)S(1)}, bf16[128,1024]{1,0:T(8,128)(2,1)S(1)}, u32[]{:S(2)}, u32[]{:S(2)}) %collective-permute-start.3) | collective-permute-done | bytes 262176 | tf_op jit(solution)/shard_map/ppermute | solution.py:325
  52.7 1.9 %collective-permute-start.5 = (bf16[128,1024]{1,0:T(8,128)(2,1)S(1)}, bf16[128,1024]{1,0:T(8,128)(2,1)S(1)}, u32[]{:S(2)}, u32[]{:S(2)}) collective-permute-start(bf16[128,1024]{1,0:T(8,128)(2,1)S(1)} %collective-permute-done.3), channel_id=1, source_target_pairs={{0,1},{1,2},{2,3},{3,0},{4,5},{5,6},{6,7},{7,4},{8,9},{9,10},{10,1... | collective-permute-start | bytes 786440 | tf_op jit(solution)/shard_map/ppermute | solution.py:328
  54.6 3.2 %collective-permute-start.6 = (bf16[256,1024]{1,0:T(8,128)(2,1)S(1)}, bf16[256,1024]{1,0:T(8,128)(2,1)S(1)}, u32[]{:S(2)}, u32[]{:S(2)}) collective-permute-start(bf16[256,1024]{1,0:T(8,128)(2,1)S(1)} %constant_dynamic-update-slice_fusion.refs_0_), channel_id=1, source_target_pairs={{0,8},{1,9},{2,10},{3,11},{4,12},{5,13},{6,14},{7,15},{8,16},{9,17... | collective-permute-start | bytes 1572872 | tf_op jit(solution)/shard_map/ppermute | solution.py:330
  57.9 3.4 %collective-permute-done.5 = bf16[128,1024]{1,0:T(8,128)(2,1)S(1)} collective-permute-done((bf16[128,1024]{1,0:T(8,128)(2,1)S(1)}, bf16[128,1024]{1,0:T(8,128)(2,1)S(1)}, u32[]{:S(2)}, u32[]{:S(2)}) %collective-permute-start.5) | collective-permute-done | bytes 262176 | tf_op jit(solution)/shard_map/ppermute | solution.py:328
  61.3 4.5 %collective-permute-start.8 = (bf16[256,1024]{1,0:T(8,128)(2,1)S(1)}, bf16[256,1024]{1,0:T(8,128)(2,1)S(1)}, u32[]{:S(2)}, u32[]{:S(2)}) collective-permute-start(bf16[256,1024]{1,0:T(8,128)(2,1)S(1)} %constant_dynamic-update-slice_fusion.5.refs_1_), channel_id=1, source_target_pairs={{0,24},{1,25},{2,26},{3,27},{4,28},{5,29},{6,30},{7,31},{8,0},{9,1... | collective-permute-start | bytes 1572872 | tf_op jit(solution)/shard_map/ppermute | solution.py:333
  65.8 2.5 %collective-permute-start.7 = (bf16[256,1024]{1,0:T(8,128)(2,1)S(1)}, bf16[256,1024]{1,0:T(8,128)(2,1)S(1)}, u32[]{:S(2)}, u32[]{:S(2)}) collective-permute-start(bf16[256,1024]{1,0:T(8,128)(2,1)S(1)} %constant_dynamic-update-slice_fusion.refs_0_), channel_id=1, source_target_pairs={{0,24},{1,25},{2,26},{3,27},{4,28},{5,29},{6,30},{7,31},{8,0},{9,1... | collective-permute-start | bytes 1572872 | tf_op jit(solution)/shard_map/ppermute | solution.py:331
  68.2 2.8 %collective-permute-start.9 = (bf16[256,1024]{1,0:T(8,128)(2,1)S(1)}, bf16[256,1024]{1,0:T(8,128)(2,1)}, u32[]{:S(2)}, u32[]{:S(2)}) collective-permute-start(bf16[256,1024]{1,0:T(8,128)(2,1)S(1)} %constant_dynamic-update-slice_fusion.5.refs_1_), channel_id=1, source_target_pairs={{0,8},{1,9},{2,10},{3,11},{4,12},{5,13},{6,14},{7,15},{8,16},{9,17... | collective-permute-start | bytes 1572872 | tf_op jit(solution)/shard_map/ppermute | solution.py:334
  71.1 1.9 %collective-permute-start.10 = (bf16[256,1024]{1,0:T(8,128)(2,1)S(1)}, bf16[256,1024]{1,0:T(8,128)(2,1)}, u32[]{:S(2)}, u32[]{:S(2)}) collective-permute-start(bf16[256,1024]{1,0:T(8,128)(2,1)S(1)} %collective-permute-done.6.refs_2_), channel_id=1, source_target_pairs={{0,8},{1,9},{2,10},{3,11},{4,12},{5,13},{6,14},{7,15},{8,16},{9,17... | collective-permute-start | bytes 1572872 | tf_op jit(solution)/shard_map/ppermute | solution.py:335
  73.0 4.6 %collective-permute-start.11 = (bf16[256,1024]{1,0:T(8,128)(2,1)S(1)}, bf16[256,1024]{1,0:T(8,128)(2,1)}, u32[]{:S(2)}, u32[]{:S(2)}) collective-permute-start(bf16[256,1024]{1,0:T(8,128)(2,1)S(1)} %collective-permute-done.8.refs_4_), channel_id=1, source_target_pairs={{0,24},{1,25},{2,26},{3,27},{4,28},{5,29},{6,30},{7,31},{8,0},{9,1... | collective-permute-start | bytes 1572872 | tf_op jit(solution)/shard_map/ppermute | solution.py:336
  77.6 11.4 %collective-permute-start.15 = (bf16[16,104,128]{2,1,0:T(8,128)(2,1)S(1)}, bf16[16,104,128]{2,1,0:T(8,128)(2,1)S(1)}, u32[]{:S(2)}, u32[]{:S(2)}) collective-permute-start(bf16[16,104,128]{2,1,0:T(8,128)(2,1)S(1)} %all-to-all-done.mine_ref), channel_id=1, source_target_pairs={{0,32},{32,0},{1,33},{33,1},{2,34},{34,2},{3,35},{35,3},{4,36},{36... | collective-permute-start | bytes 1277960 | tf_op jit(solution)/shard_map/ppermute | solution.py:322
  89.0 1.8 %shard_map.69 = (f32[16,240,128]{2,1,0:T(8,128)S(1)}, f32[2,16,128]{2,1,0:T(8,128)S(1)}) custom-call(bf16[16,104,128]{2,1,0:T(8,128)(2,1)S(1)} %all-to-all-done.mine_ref), custom_call_target="tpu_custom_call" | custom-call | tf_op jit(solution)/shard_map/pallas_call | solution.py:270
  91.1 2.2 %shard_map.70.refs_6_ = f32[200,1024]{1,0:T(8,128)S(1)} custom-call(bf16[256,1024]{1,0:T(8,128)(2,1)S(1)} %constant_dynamic-update-slice_fusion.refs_0_, bf16[256,1024]{1,0:T(8,128)(2,1)S(1)} %constant_dynamic-update-slice_fusion.5.refs_1_, bf16[256,1024]{1,0:T(8,128)(2,1)S(1)} %collective-permute-done.6.refs_2_, ...), custom_call_target="tpu_custom_call" | custom-call | tf_op jit(solution)/shard_map/pallas_call | solution.py:270
  93.3 3.0 %shard_map.71.refs_11_ = bf16[200,1024]{1,0:T(8,128)(2,1)S(1)} custom-call(bf16[256,1024]{1,0:T(8,128)(2,1)} %collective-permute-done.9.refs_0_.refs_5_, bf16[256,1024]{1,0:T(8,128)(2,1)} %collective-permute-done.10.refs_1_.refs_6_, bf16[256,1024]{1,0:T(8,128)(2,1)} %collective-permute-done.11.refs_2_.refs_7_, ...), custom_call_target="tpu_custom_call" | custom-call | tf_op jit(solution)/shard_map/pallas_call | solution.py:270
  96.3 3.4 %collective-permute-start.16 = (bf16[200,1024]{1,0:T(8,128)(2,1)S(1)}, bf16[200,1024]{1,0:T(8,128)(2,1)S(1)}, u32[]{:S(2)}, u32[]{:S(2)}) collective-permute-start(bf16[200,1024]{1,0:T(8,128)(2,1)S(1)} %shard_map.71.refs_11_), channel_id=1, source_target_pairs={{0,32},{32,0},{1,33},{33,1},{2,34},{34,2},{3,35},{35,3},{4,36},{36... | collective-permute-start | bytes 1228808 | tf_op jit(solution)/shard_map/ppermute | solution.py:350
  99.7 1.4 %collective-permute-done.16.refs_12_ = bf16[200,1024]{1,0:T(8,128)(2,1)S(1)} collective-permute-done((bf16[200,1024]{1,0:T(8,128)(2,1)S(1)}, bf16[200,1024]{1,0:T(8,128)(2,1)S(1)}, u32[]{:S(2)}, u32[]{:S(2)}) %collective-permute-start.16) | collective-permute-done | bytes 409632 | tf_op jit(solution)/shard_map/ppermute | solution.py:350
  101.1 4.6 %shard_map.72 = (f32[8,64,128]{2,1,0:T(8,128)S(1)}, bf16[8,64,128]{2,1,0:T(8,128)(2,1)S(1)}) custom-call(bf16[256,1024]{1,0:T(8,128)(2,1)S(1)} %constant_dynamic-update-slice_fusion.refs_0_, bf16[256,1024]{1,0:T(8,128)(2,1)S(1)} %constant_dynamic-update-slice_fusion.5.refs_1_, bf16[256,1024]{1,0:T(8,128)(2,1)S(1)} %collective-permute-done.6.refs_2_, ...), custom_call_target="tpu_custom_call" | custom-call | tf_op jit(solution)/shard_map/pallas_call | solution.py:270
  105.7 2.3 %collective-permute-start.17 = (bf16[8,64,128]{2,1,0:T(8,128)(2,1)S(1)}, bf16[8,64,128]{2,1,0:T(8,128)(2,1)S(1)}, u32[]{:S(2)}, u32[]{:S(2)}) collective-permute-start(bf16[8,64,128]{2,1,0:T(8,128)(2,1)S(1)} %get-tuple-element.18), channel_id=1, source_target_pairs={{0,32},{32,0},{1,33},{33,1},{2,34},{34,2},{3,35},{35,3},{4,36},{36... | collective-permute-start | bytes 393224 | tf_op jit(solution)/shard_map/ppermute | solution.py:354
  108.0 1.0 collective-permute-done.17.got_ref
  109.0 19.7 %all_to_all.10.back_ref = bf16[8,64,128]{2,1,0:T(8,128)(2,1)S(1)} all-to-all(bf16[8,64,128]{2,1,0:T(8,128)(2,1)S(1)} %shard_map.73), channel_id=1, replica_groups=mesh['zl'=8,'core'=2,'y'=4,'zh'=2,'x'=4] {'zl'}, dimensions={0} | all-to-all | bytes 262144 | tf_op jit(solution)/shard_map/all_to_all | solution.py:356
  (40 shorter events, 3.2 us)
Async XLA Ops:
  0.0 31.8 %copy-start.5 = (f32[256]{0:T(256)S(1)}, f32[256]{0:T(256)}, u32[]{:S(2)}) copy-start(f32[256]{0:T(256)} %param.11) | copy-start | bytes 3076
  0.0 31.8 %copy-start.3 = (f32[256,8]{0,1:T(8,128)S(1)}, f32[256,8]{0,1:T(8,128)}, u32[]{:S(2)}) copy-start(f32[256,8]{0,1:T(8,128)} %param.9) | copy-start | bytes 24580
  0.0 31.8 %copy-start.4 = (f32[256]{0:T(256)S(1)}, f32[256]{0:T(256)}, u32[]{:S(2)}) copy-start(f32[256]{0:T(256)} %param.8) | copy-start | bytes 3076
  0.8 10.9 %collective-permute-start = (bf16[16,1024]{1,0:T(8,128)(2,1)S(1)}, bf16[16,1024]{1,0:T(8,128)(2,1)S(1)}, u32[]{:S(2)}, u32[]{:S(2)}) collective-permute-start(bf16[16,1024]{1,0:T(8,128)(2,1)S(1)} %get-tuple-element.20), channel_id=1, source_target_pairs={{0,256},{64,320},{128,384},{192,448},{256,0},{320,64},{384,128},{4... | collective-permute-start | bytes 98312 | tf_op jit(solution)/shard_map/ppermute | solution.py:286
  11.7 15.9 %collective-permute-start.1 = (bf16[32,1024]{1,0:T(8,128)(2,1)S(1)}, bf16[32,1024]{1,0:T(8,128)(2,1)S(1)}, u32[]{:S(2)}, u32[]{:S(2)}) collective-permute-start(bf16[32,1024]{1,0:T(8,128)(2,1)S(1)} %pad_maximum_fusion.2), channel_id=1, source_target_pairs={{0,128},{64,192},{128,0},{192,64},{256,384},{320,448},{384,256},{4... | collective-permute-start | bytes 196616 | tf_op jit(solution)/shard_map/ppermute | solution.py:286
  16.6 0.9 copy-start
  17.5 0.8 copy-start.2
  18.3 4.7 %collective-permute-start.12 = (bf16[160,128]{1,0:T(8,128)(2,1)S(1)}, bf16[160,128]{1,0:T(8,128)(2,1)S(1)}, u32[]{:S(2)}, u32[]{:S(2)}) collective-permute-start(bf16[160,128]{1,0:T(8,128)(2,1)S(1)} %shard_map.65), channel_id=1, source_target_pairs={{4,12},{5,13},{6,14},{7,15},{8,0},{9,1},{10,2},{11,3},{12,20},{13,... | collective-permute-start | bytes 122888 | tf_op jit(solution)/shard_map/ppermute | solution.py:296
  23.2 8.5 %collective-permute-start.13 = (bf16[80,128]{1,0:T(8,128)(2,1)S(1)}, bf16[80,128]{1,0:T(8,128)(2,1)S(1)}, u32[]{:S(2)}, u32[]{:S(2)}) collective-permute-start(bf16[80,128]{1,0:T(8,128)(2,1)S(1)} %get-tuple-element.13), channel_id=1, source_target_pairs={{0,1},{1,2},{2,3},{4,5},{5,6},{6,7},{8,9},{9,10},{10,11},{12,13},{... | collective-permute-start | bytes 61448 | tf_op jit(solution)/shard_map/ppermute | solution.py:307
  26.4 5.4 %collective-permute-start.14 = (bf16[80,128]{1,0:T(8,128)(2,1)S(1)}, bf16[80,128]{1,0:T(8,128)(2,1)S(1)}, u32[]{:S(2)}, u32[]{:S(2)}) collective-permute-start(bf16[80,128]{1,0:T(8,128)(2,1)S(1)} %get-tuple-element.14), channel_id=1, source_target_pairs={{1,0},{2,1},{3,2},{5,4},{6,5},{7,6},{9,8},{10,9},{11,10},{13,12},{... | collective-permute-start | bytes 61448 | tf_op jit(solution)/shard_map/ppermute | solution.py:308
  27.7 15.8 %collective-permute-start.2 = (bf16[64,1024]{1,0:T(8,128)(2,1)S(1)}, bf16[64,1024]{1,0:T(8,128)(2,1)S(1)}, u32[]{:S(2)}, u32[]{:S(2)}) collective-permute-start(bf16[64,1024]{1,0:T(8,128)(2,1)S(1)} %pad_maximum_fusion.1), channel_id=1, source_target_pairs={{0,64},{64,0},{128,192},{192,128},{256,320},{320,256},{384,448},{4... | collective-permute-start | bytes 393224 | tf_op jit(solution)/shard_map/ppermute | solution.py:286
  33.3 44.4 %all-to-all-start = ((bf16[16,104,128]{2,1,0:T(8,128)(2,1)}), bf16[16,104,128]{2,1,0:T(8,128)(2,1)S(1)}, u32[]{:S(2)}, u32[]{:S(2)}) async-start(bf16[16,104,128]{2,1,0:T(8,128)(2,1)} %shard_map.67), calls=%async_computation | async-start | bytes 851968 | tf_op jit(solution)/shard_map/all_to_all | solution.py:321
  43.5 9.1 %collective-permute-start.3 = (bf16[128,1024]{1,0:T(8,128)(2,1)S(1)}, bf16[128,1024]{1,0:T(8,128)(2,1)S(1)}, u32[]{:S(2)}, u32[]{:S(2)}) collective-permute-start(bf16[128,1024]{1,0:T(8,128)(2,1)S(1)} %pad_maximum_fusion), channel_id=1, source_target_pairs={{0,1},{1,2},{2,3},{3,0},{4,5},{5,6},{6,7},{7,4},{8,9},{9,10},{10,1... | collective-permute-start | bytes 786440 | tf_op jit(solution)/shard_map/ppermute | solution.py:325
  47.5 10.3 %collective-permute-start.4 = (bf16[128,1024]{1,0:T(8,128)(2,1)S(1)}, bf16[128,1024]{1,0:T(8,128)(2,1)S(1)}, u32[]{:S(2)}, u32[]{:S(2)}) collective-permute-start(bf16[128,1024]{1,0:T(8,128)(2,1)S(1)} %pad_maximum_fusion), channel_id=1, source_target_pairs={{0,3},{1,0},{2,1},{3,2},{4,7},{5,4},{6,5},{7,6},{8,11},{9,8},{10,9... | collective-permute-start | bytes 786440 | tf_op jit(solution)/shard_map/ppermute | solution.py:326
  52.7 8.6 %collective-permute-start.5 = (bf16[128,1024]{1,0:T(8,128)(2,1)S(1)}, bf16[128,1024]{1,0:T(8,128)(2,1)S(1)}, u32[]{:S(2)}, u32[]{:S(2)}) collective-permute-start(bf16[128,1024]{1,0:T(8,128)(2,1)S(1)} %collective-permute-done.3), channel_id=1, source_target_pairs={{0,1},{1,2},{2,3},{3,0},{4,5},{5,6},{6,7},{7,4},{8,9},{9,10},{10,1... | collective-permute-start | bytes 786440 | tf_op jit(solution)/shard_map/ppermute | solution.py:328
  54.6 16.4 %collective-permute-start.6 = (bf16[256,1024]{1,0:T(8,128)(2,1)S(1)}, bf16[256,1024]{1,0:T(8,128)(2,1)S(1)}, u32[]{:S(2)}, u32[]{:S(2)}) collective-permute-start(bf16[256,1024]{1,0:T(8,128)(2,1)S(1)} %constant_dynamic-update-slice_fusion.refs_0_), channel_id=1, source_target_pairs={{0,8},{1,9},{2,10},{3,11},{4,12},{5,13},{6,14},{7,15},{8,16},{9,17... | collective-permute-start | bytes 1572872 | tf_op jit(solution)/shard_map/ppermute | solution.py:330
  61.3 11.7 %collective-permute-start.8 = (bf16[256,1024]{1,0:T(8,128)(2,1)S(1)}, bf16[256,1024]{1,0:T(8,128)(2,1)S(1)}, u32[]{:S(2)}, u32[]{:S(2)}) collective-permute-start(bf16[256,1024]{1,0:T(8,128)(2,1)S(1)} %constant_dynamic-update-slice_fusion.5.refs_1_), channel_id=1, source_target_pairs={{0,24},{1,25},{2,26},{3,27},{4,28},{5,29},{6,30},{7,31},{8,0},{9,1... | collective-permute-start | bytes 1572872 | tf_op jit(solution)/shard_map/ppermute | solution.py:333
  65.8 25.3 %collective-permute-start.7 = (bf16[256,1024]{1,0:T(8,128)(2,1)S(1)}, bf16[256,1024]{1,0:T(8,128)(2,1)S(1)}, u32[]{:S(2)}, u32[]{:S(2)}) collective-permute-start(bf16[256,1024]{1,0:T(8,128)(2,1)S(1)} %constant_dynamic-update-slice_fusion.refs_0_), channel_id=1, source_target_pairs={{0,24},{1,25},{2,26},{3,27},{4,28},{5,29},{6,30},{7,31},{8,0},{9,1... | collective-permute-start | bytes 1572872 | tf_op jit(solution)/shard_map/ppermute | solution.py:331
  68.2 25.0 %collective-permute-start.9 = (bf16[256,1024]{1,0:T(8,128)(2,1)S(1)}, bf16[256,1024]{1,0:T(8,128)(2,1)}, u32[]{:S(2)}, u32[]{:S(2)}) collective-permute-start(bf16[256,1024]{1,0:T(8,128)(2,1)S(1)} %constant_dynamic-update-slice_fusion.5.refs_1_), channel_id=1, source_target_pairs={{0,8},{1,9},{2,10},{3,11},{4,12},{5,13},{6,14},{7,15},{8,16},{9,17... | collective-permute-start | bytes 1572872 | tf_op jit(solution)/shard_map/ppermute | solution.py:334
  71.1 22.2 %collective-permute-start.10 = (bf16[256,1024]{1,0:T(8,128)(2,1)S(1)}, bf16[256,1024]{1,0:T(8,128)(2,1)}, u32[]{:S(2)}, u32[]{:S(2)}) collective-permute-start(bf16[256,1024]{1,0:T(8,128)(2,1)S(1)} %collective-permute-done.6.refs_2_), channel_id=1, source_target_pairs={{0,8},{1,9},{2,10},{3,11},{4,12},{5,13},{6,14},{7,15},{8,16},{9,17... | collective-permute-start | bytes 1572872 | tf_op jit(solution)/shard_map/ppermute | solution.py:335
  73.0 20.2 %collective-permute-start.11 = (bf16[256,1024]{1,0:T(8,128)(2,1)S(1)}, bf16[256,1024]{1,0:T(8,128)(2,1)}, u32[]{:S(2)}, u32[]{:S(2)}) collective-permute-start(bf16[256,1024]{1,0:T(8,128)(2,1)S(1)} %collective-permute-done.8.refs_4_), channel_id=1, source_target_pairs={{0,24},{1,25},{2,26},{3,27},{4,28},{5,29},{6,30},{7,31},{8,0},{9,1... | collective-permute-start | bytes 1572872 | tf_op jit(solution)/shard_map/ppermute | solution.py:336
  77.6 13.2 %collective-permute-start.15 = (bf16[16,104,128]{2,1,0:T(8,128)(2,1)S(1)}, bf16[16,104,128]{2,1,0:T(8,128)(2,1)S(1)}, u32[]{:S(2)}, u32[]{:S(2)}) collective-permute-start(bf16[16,104,128]{2,1,0:T(8,128)(2,1)S(1)} %all-to-all-done.mine_ref), channel_id=1, source_target_pairs={{0,32},{32,0},{1,33},{33,1},{2,34},{34,2},{3,35},{35,3},{4,36},{36... | collective-permute-start | bytes 1277960 | tf_op jit(solution)/shard_map/ppermute | solution.py:322
  96.3 32.4 %copy-start.1 = (bf16[64,8,128]{2,1,0:T(8,128)(2,1)S(1)}, bf16[64,8,128]{2,1,0:T(8,128)(2,1)}, u32[]{:S(2)}) copy-start(bf16[64,8,128]{2,1,0:T(8,128)(2,1)} %param.6) | copy-start | bytes 393220
  96.3 4.7 %collective-permute-start.16 = (bf16[200,1024]{1,0:T(8,128)(2,1)S(1)}, bf16[200,1024]{1,0:T(8,128)(2,1)S(1)}, u32[]{:S(2)}, u32[]{:S(2)}) collective-permute-start(bf16[200,1024]{1,0:T(8,128)(2,1)S(1)} %shard_map.71.refs_11_), channel_id=1, source_target_pairs={{0,32},{32,0},{1,33},{33,1},{2,34},{34,2},{3,35},{35,3},{4,36},{36... | collective-permute-start | bytes 1228808 | tf_op jit(solution)/shard_map/ppermute | solution.py:350
  105.7 3.3 %collective-permute-start.17 = (bf16[8,64,128]{2,1,0:T(8,128)(2,1)S(1)}, bf16[8,64,128]{2,1,0:T(8,128)(2,1)S(1)}, u32[]{:S(2)}, u32[]{:S(2)}) collective-permute-start(bf16[8,64,128]{2,1,0:T(8,128)(2,1)S(1)} %get-tuple-element.18), channel_id=1, source_target_pairs={{0,32},{32,0},{1,33},{33,1},{2,34},{34,2},{3,35},{35,3},{4,36},{36... | collective-permute-start | bytes 393224 | tf_op jit(solution)/shard_map/ppermute | solution.py:354
